TPU v7x, 32 devices: a whole 2x2x4 slice. The times are simulated.
32 devices in a mesh: groups: 2 (over x), ctx: 16 (over z, y, core).
Axes of the slice: x: 2, y: 2, z: 4, core: 2. Of those that a mesh axis runs over, the one named last changes fastest.
Arguments:
- features: bfloat16 [32768, 1024], P(('groups', 'ctx')), parts along dimension 0, may hold values from -6 to 6
- write_map: bfloat16 [32768, 128], P(('groups', 'ctx')), parts along dimension 0, may hold values from -6 to 6
- read_map: bfloat16 [32768, 128], P(('groups', 'ctx')), parts along dimension 0, may hold values from -3 to 3
- step_raw: float32 [32768, 16], P(('groups', 'ctx')), parts along dimension 0, may hold values from -3 to 3
- tokens: int32 [32768], P(('groups', 'ctx')), parts along dimension 0, may hold values from 0 to 4
- base_shift: float32 [5, 16], replicated, may hold values from -8 to -2
- decay_rate: float32 [16], replicated, may hold values from 0 to 2, as said below
- skip_gain: float32 [16], replicated, may hold values from 0.5 to 1.5
- cotangent: bfloat16 [32768, 1024], P(('groups', 'ctx')), parts along dimension 0, may hold values from -20 to 20
Outputs:
- layer_out: bfloat16 [32768, 1024], P(('groups', 'ctx')), parts along dimension 0
- grad_feature: bfloat16 [32768, 1024], P(('groups', 'ctx')), parts along dimension 0
- grad_write: bfloat16 [32768, 128], P(('groups', 'ctx')), parts along dimension 0
- grad_read: bfloat16 [32768, 128], P(('groups', 'ctx')), parts along dimension 0
- grad_step: float32 [32768, 16], P(('groups', 'ctx')), parts along dimension 0
- grad_skip: float32 [32], P('groups'), parts along dimension 0
There are 2 independent parts, one for each index of `groups`. A program takes and returns all parts, laid end to end along the dimension named above; an argument that names none is the same for every part. Nothing has to cross between parts.
Inputs may be any that keep to these rules, and one draw needn't show every extreme that they name: `tokens`: 0, 1, 2, 3 stand for the bases A, C, G, T and 4 for an unknown base N. `decay_rate`: positive.
All inputs are finite; a program needn't handle non-finite values.
Results may differ from a plain program's by a relative error of at most 0.0015.
Values sent between devices are 32-bit elements; how exact they have to be, the bound alone decides.
A program may use at most 704 MiB of HBM per device.

v0:
```python
import math

import jax
import jax.numpy as jnp
from jax import lax
from jax.sharding import PartitionSpec as P

SPAN = 256


PRECISE = lax.Precision.HIGHEST
MASKED = 10000.0


def entering(part, axis, combine, identity, reverse):
    count = lax.axis_size(axis)
    place = lax.axis_index(axis)
    ahead = count - 1 - place if reverse else place
    gathered = jax.tree.map(lambda a: lax.all_gather(a, axis), part)
    state = jax.tree.map(lambda a, e: jnp.zeros_like(a) + jnp.asarray(e, a.dtype), part, identity)

    def one(turn, state):
        source = count - 1 - turn if reverse else turn
        return combine(
            state, jax.tree.map(lambda a: lax.dynamic_index_in_dim(a, source, 0, False), gathered)
        )

    return lax.fori_loop(0, ahead, one, state)


def step_rates(step_raw, base_shift, tokens):
    base_codes = jnp.arange(5, dtype=jnp.int32)
    onehot = (tokens[:, None] == base_codes[None, :]).astype(jnp.float32)
    paired = jnp.where(tokens < 4, 3 - tokens, tokens)
    onehot_rc = (paired[:, None] == base_codes[None, :]).astype(jnp.float32)
    step_fwd = jax.nn.softplus(step_raw + jnp.dot(onehot, base_shift, precision=PRECISE))
    step_rc = jax.nn.softplus(
        step_raw + jnp.dot(onehot_rc, jnp.flip(base_shift, 1), precision=PRECISE)
    )
    return (step_fwd, step_rc)


def decay_parts(step_sizes, rate_vec, block_len):
    row_count, head_count = step_sizes.shape
    steps_blocked = step_sizes.reshape(row_count // block_len, block_len, head_count)
    running = jnp.cumsum(steps_blocked * rate_vec[None, None, :], axis=1)
    return (steps_blocked, running, jnp.exp(-running[:, -1]))


def block_parts(values, writes, step_sizes, rate_vec, block_len):
    steps_blocked, running, fades = decay_parts(step_sizes, rate_vec, block_len)
    block_count = steps_blocked.shape[0]
    value_blocks = values.reshape((block_count, block_len) + values.shape[1:])
    write_blocks = writes.reshape(block_count, block_len, writes.shape[1])
    tail_weight = jnp.exp(running - running[:, -1:]) * steps_blocked
    block_states = jnp.einsum(
        "ksh,kshp,ksn->khpn", tail_weight, value_blocks, write_blocks, precision=PRECISE
    )
    return (value_blocks, write_blocks, steps_blocked, running, fades, block_states)


def summary(values, writes, step_sizes, rate_vec, block_len):
    parts = block_parts(values, writes, step_sizes, rate_vec, block_len)
    fades, block_states = (parts[4], parts[5])
    memory = jnp.zeros_like(block_states[0])
    product = jnp.ones_like(fades[0])
    for block in range(fades.shape[0]):
        memory = fades[block][:, None, None] * memory + block_states[block]
        product = product * fades[block]
    return (product, memory)


def emit(values, writes, reads, step_sizes, rate_vec, entry, block_len):
    value_blocks, write_blocks, steps_blocked, running, fades, block_states = block_parts(
        values, writes, step_sizes, rate_vec, block_len
    )
    block_count = fades.shape[0]
    read_blocks = reads.reshape(block_count, block_len, reads.shape[1])
    starts = [entry]
    for block in range(block_count - 1):
        starts.append(fades[block][:, None, None] * starts[-1] + block_states[block])
    start_states = jnp.stack(starts)
    causal = jnp.tril(jnp.ones((block_len, block_len), dtype=jnp.bool_))
    scores = jnp.einsum("ktn,ksn->kts", read_blocks, write_blocks, precision=PRECISE)

    def one_head(pieces):
        run_head, step_head, value_head = pieces
        spread = run_head[:, :, None] - run_head[:, None, :]
        fade_matrix = jnp.exp(-jnp.where(causal[None], spread, MASKED))
        weights = fade_matrix * scores * step_head[:, None, :]
        return jnp.einsum("kts,ksp->ktp", weights, value_head, precision=PRECISE)

    per_head = lax.map(
        jax.checkpoint(one_head),
        (
            jnp.transpose(running, (2, 0, 1)),
            jnp.transpose(steps_blocked, (2, 0, 1)),
            jnp.transpose(value_blocks, (2, 0, 1, 3)),
        ),
    )
    inner = jnp.transpose(per_head, (1, 2, 0, 3))
    carried = jnp.exp(-running)[..., None] * jnp.einsum(
        "ktn,khpn->kthp", read_blocks, start_states, precision=PRECISE
    )
    return (inner + carried).reshape(values.shape)


def adjoint(cotangents, reads, step_sizes, rate_vec, block_len):
    steps_blocked, running, fades = decay_parts(step_sizes, rate_vec, block_len)
    block_count = fades.shape[0]
    before = [jnp.ones_like(fades[0])]
    for block in range(block_count - 1):
        before.append(before[-1] * fades[block])
    factors = jnp.exp(-running) * jnp.stack(before)[:, None, :]
    cot_blocks = cotangents.reshape((block_count, block_len) + cotangents.shape[1:])
    read_blocks = reads.reshape(block_count, block_len, reads.shape[1])
    return jnp.einsum("kth,kthp,ktn->hpn", factors, cot_blocks, read_blocks, precision=PRECISE)


def link(earlier, later):
    return (earlier[0] * later[0], later[0][:, None, None] * earlier[1] + later[1])


def link_pairs(earlier, later):
    return link((earlier[0], earlier[1]), (later[0], later[1])) + link(
        (earlier[2], earlier[3]), (later[2], later[3])
    )


def flip_rows(array):
    return jnp.flip(array, 0)


def per_device(
    features, write_map, read_map, step_raw, tokens, base_shift, decay_rate, skip_gain, cotangent
):
    row_count, width_all = features.shape
    head_count = decay_rate.shape[0]
    head_size = width_all // head_count
    state_size = write_map.shape[1]
    block_len = min(SPAN, row_count)
    values = features.astype(jnp.float32).reshape(row_count, head_count, head_size)
    writes = write_map.astype(jnp.float32)
    reads = read_map.astype(jnp.float32)
    cot_heads = cotangent.astype(jnp.float32).reshape(row_count, head_count, head_size)
    rev_rates = jnp.flip(decay_rate)

    def sums_fn(value_in, write_in, raw_in):
        step_fwd, step_rc = step_rates(raw_in, base_shift, tokens)
        lam_fwd, zone_fwd = summary(value_in, write_in, step_fwd, decay_rate, block_len)
        lam_rc, zone_rc = summary(
            flip_rows(value_in), flip_rows(write_in), flip_rows(step_rc), rev_rates, block_len
        )
        return (lam_fwd, zone_fwd, lam_rc, zone_rc)

    (lam_fwd, zone_fwd, lam_rc, zone_rc), pull_sums = jax.vjp(sums_fn, values, writes, step_raw)
    step_fwd, step_rc = step_rates(step_raw, base_shift, tokens)
    adj_fwd = adjoint(cot_heads, reads, step_fwd, decay_rate, block_len)
    adj_rc = adjoint(
        flip_rows(cot_heads), flip_rows(reads), flip_rows(step_rc), rev_rates, block_len
    )
    unit_rates = jnp.ones((head_count,), jnp.float32)
    empty_state = jnp.zeros((head_count, head_size, state_size), jnp.float32)
    ahead = entering(
        (lam_fwd, zone_fwd, lam_rc, adj_rc),
        "ctx",
        link_pairs,
        (unit_rates, empty_state, unit_rates, empty_state),
        False,
    )
    behind = entering(
        (lam_rc, zone_rc, lam_fwd, adj_fwd),
        "ctx",
        link_pairs,
        (unit_rates, empty_state, unit_rates, empty_state),
        True,
    )
    enter_fwd, back_rc = (ahead[1], ahead[3])
    enter_rc, back_fwd = (behind[1], behind[3])

    def mixed_fn(value_in, write_in, read_in, raw_in, gain_in):
        fwd_steps, rc_steps = step_rates(raw_in, base_shift, tokens)
        y_fwd = emit(value_in, write_in, read_in, fwd_steps, decay_rate, enter_fwd, block_len)
        y_rc = flip_rows(
            emit(
                flip_rows(value_in),
                flip_rows(write_in),
                flip_rows(read_in),
                flip_rows(rc_steps),
                rev_rates,
                enter_rc,
                block_len,
            )
        )
        return y_fwd + y_rc + (gain_in + jnp.flip(gain_in))[None, :, None] * value_in

    mixed, pull_mixed = jax.vjp(mixed_fn, values, writes, reads, step_raw, skip_gain)
    d_lam_fwd = jnp.sum(back_fwd * enter_fwd, axis=(1, 2))
    d_lam_rc = jnp.sum(back_rc * enter_rc, axis=(1, 2))
    grad_x_sum, grad_w_sum, grad_s_sum = pull_sums((d_lam_fwd, back_fwd, d_lam_rc, back_rc))
    grad_x_mix, grad_w_mix, grad_r_mix, grad_s_mix, grad_g_mix = pull_mixed(cot_heads)
    gain_total = lax.psum(grad_g_mix, "ctx")
    length_all = row_count * lax.axis_size("ctx")
    norm_scale = 1.0 / math.sqrt(length_all * head_size)
    return (
        mixed.reshape(row_count, width_all).astype(jnp.bfloat16),
        (grad_x_sum + grad_x_mix).reshape(row_count, width_all).astype(jnp.bfloat16),
        (grad_w_sum + grad_w_mix).astype(jnp.bfloat16),
        grad_r_mix.astype(jnp.bfloat16),
        grad_s_sum + grad_s_mix,
        gain_total * norm_scale,
    )


def solution(mesh):
    in_specs = (
        P(("groups", "ctx"), None),
        P(("groups", "ctx"), None),
        P(("groups", "ctx"), None),
        P(("groups", "ctx"), None),
        P(("groups", "ctx")),
        P(),
        P(),
        P(),
        P(("groups", "ctx"), None),
    )
    out_specs = (
        P(("groups", "ctx"), None),
        P(("groups", "ctx"), None),
        P(("groups", "ctx"), None),
        P(("groups", "ctx"), None),
        P(("groups", "ctx"), None),
        P("groups"),
    )
    return jax.shard_map(
        per_device, mesh=mesh, in_specs=in_specs, out_specs=out_specs, check_vma=False
    )
```

profile of v0, /device:TPU:0, one launch (start us, length us, event | category | flops | bytes accessed | tf_op | source)
XLA Modules:
  0.0 1037.4 jit_solution(3101822996276380419)
XLA Ops:
  28.4 3.9 copy.368
  32.3 5.1 reshape.483
  38.8 3.9 fusion.84
  48.6 4.1 convert_element_type.37
  53.5 7.3 rev.78
  60.8 5.6 reshape.451
  69.8 4.3 fusion.114
  86.8 7.3 rev.81
  94.7 5.9 fusion.86
  113.5 5.7 reshape.456
  120.8 5.0 copy.354
  134.3 202.3 %while.104 = (s32[]{:T(128)}, f32[4,256,256]{2,1,0:T(8,128)}, f32[16,4,256]{2,0,1:T(8,128)}, f32[16,4,256]{2,0,1:T(8,128)}, f32[16,4,256,64]{2,3,0,1:T(8,128)}, ...) while((s32[]{:T(128)}, f32[4,256,256]{2,1,0:T(8,128)}, ...), condition=%wide.region_20.22_spmd.clone, body=%wide.region_16.21_spmd.clone.sunk | while | flops 408222720 | bytes 7106739 | solution.py:93
  149.5 4.1 fusion.270
  162.2 4.1 fusion.270
  174.9 4.1 fusion.270
  187.5 4.1 fusion.270
  200.2 4.1 fusion.270
  212.8 4.1 fusion.270
  225.5 4.1 fusion.270
  238.1 4.1 fusion.270
  250.7 4.1 fusion.270
  263.4 4.1 fusion.270
  276.1 4.1 fusion.270
  288.9 4.1 fusion.270
  301.5 4.1 fusion.270
  314.1 4.1 fusion.270
  326.7 4.1 fusion.270
  340.5 143.3 %while.105 = (s32[]{:T(128)}, f32[4,256,256]{2,1,0:T(8,128)S(1)}, f32[16,4,256]{2,0,1:T(8,128)S(1)}, f32[16,4,256]{2,0,1:T(8,128)S(1)}, f32[16,4,256,64]{2,3,0,1...) while((s32[]{:T(128)}, f32[4,256,256]{2,1,0:T(8,128)S(1)}, ...), condition=%wide.region_25.27_spmd.clone, body=%wide.region_21.26_spmd.clone.sunk | while | flops 408222720 | bytes 7106739 | solution.py:93
  484.9 9.2 fusion.107
  494.1 3.9 convolution_add_fusion.3
  498.0 36.6 %psum.7 = f32[16]{0:T(128)} all-reduce(f32[16]{0:T(128)} %add_any.333), channel_id=1, replica_groups=mesh['groups'=2,'ctx'=16] {'ctx'}, use_global_device_ids=true, to_apply=%region_58.60 | all-reduce | flops 16 | bytes 128 | tf_op jit(solution)/shard_map/psum | solution.py:202
  536.9 4.7 rev.87
  541.7 17.9 %all-gather.3 = f32[16,1,16]{2,1,0:T(1,128)} all-gather(f32[1,1,16]{2,1,0:T(1,128)} %get-tuple-element.1391), channel_id=1, replica_groups=mesh['groups'=2,'ctx'=16] {'ctx'}, dimensions={0}, use_global_device_ids=true | all-gather | bytes 1088 | tf_op jit(solution)/shard_map/all_gather | solution.py:19
  559.6 19.8 %all-gather.2 = f32[16,1,16]{2,1,0:T(1,128)} all-gather(f32[1,1,16]{2,1,0:T(1,128)} %get-tuple-element.1396), channel_id=1, replica_groups=mesh['groups'=2,'ctx'=16] {'ctx'}, dimensions={0}, use_global_device_ids=true | all-gather | bytes 1088 | tf_op jit(solution)/shard_map/all_gather | solution.py:19
  581.2 8.2 fusion.110
  595.2 5.5 convolution_bitcast_fusion.5
  603.2 60.3 %while.102 = (s32[]{:T(128)}, f32[16,4,256,64]{2,3,0,1:T(8,128)}, f32[16,4,256]{2,1,0:T(4,128)}, f32[4,256,256]{2,1,0:T(8,128)S(1)}, f32[16,4,256]{2,1,0:T(4,128...) while((s32[]{:T(128)}, f32[16,4,256,64]{2,3,0,1:T(8,128)}, ...), condition=%wide.region_3.5_spmd.clone, body=%wide.region_2.4_spmd.clone.sunk | while | flops 202637312 | bytes 1668193 | solution.py:93
  665.9 65.4 %while.103 = (s32[]{:T(128)}, f32[16,4,256,64]{2,3,0,1:T(8,128)}, f32[16,4,256]{2,1,0:T(4,128)}, f32[4,256,256]{2,1,0:T(8,128)}, f32[16,4,256]{2,1,0:T(4,128)}, ...) while((s32[]{:T(128)}, f32[16,4,256,64]{2,3,0,1:T(8,128)}, ...), condition=%wide.region_11.13_spmd.clone, body=%wide.region_10.12_spmd.clone.sunk | while | flops 202637312 | bytes 1668193 | solution.py:93
  731.6 42.0 %while.101 = (s32[]{:T(128)}, f32[16,64,128]{2,1,0:T(8,128)S(1)}, f32[16,64,128]{2,1,0:T(8,128)S(1)}, s32[]{:T(128)}, f32[16,16]{1,0:T(8,128)}, /*index=5*/f32[1...) while((s32[]{:T(128)}, f32[16,64,128]{2,1,0:T(8,128)S(1)}, ...), condition=%wide.region_15.17_spmd, body=%wide.region_14.16_spmd.sunk | while | flops 524294 | bytes 3146295 | solution.py:28
  773.6 4.3 fusion.130
  778.0 7.5 fusion.92
  785.5 5.4 convolution_bitcast_fusion.7
  792.6 7.6 fusion.83
  810.0 4.7 rev.86
  814.7 15.6 %fusion.68 = (f32[4,256,16]{1,0,2:T(4,128)S(1)}, f32[4,256,16]{1,0,2:T(4,128)S(1)}) fusion(bf16[4,256,16,64]{1,0,3,2:T(4,128)(2,1)} %reshape_reshape.11, f32[4,256,16,64]{1,3,2,0:T(8,128)} %convolution_bitcast_fusion.6, f32[4,256,16,64]{1,3,2,0:T(8,128)} %convolution_bitcast_fusion.4), kind=kLoop, calls=%fused_computation.102 | loop fusion | flops 5210112 | bytes 10616832
  830.4 10.2 multiply_reduce_fusion.3
  847.1 11.2 %reduce-window.70 = f32[4,16,2,128]{3,1,2,0:T(8,128)} reduce-window(f32[4,16,2,128]{3,1,2,0:T(8,128)} %copy_bitcast_fusion.4, f32[]{:T(128)} %constant.254.clone.1), window={size=1x1x1x128 pad=0_0x0_0x0_0x0_127}, to_apply=%region_40.42 | reduce-window | flops 2080768 | bytes 131076 | tf_op jit(solution)/shard_map/reduce-window.10
  866.7 11.4 %reduce-window.66 = f32[4,16,2,128]{3,1,2,0:T(8,128)} reduce-window(f32[4,16,2,128]{3,1,2,0:T(8,128)} %copy_bitcast_fusion.5, f32[]{:T(128)} %constant.254.clone.1), window={size=1x1x1x128 pad=0_0x0_0x0_0x0_127}, to_apply=%region_32.34 | reduce-window | flops 2080768 | bytes 131076 | tf_op jit(solution)/shard_map/reduce-window.8
  881.1 10.3 fusion.108
  891.4 5.7 fusion.77
  901.3 6.9 fusion.109
  913.1 8.6 multiply_bitcast_fusion.1
  924.3 7.3 rev.84
  931.6 4.8 copy.585
  936.4 7.3 rev.85
  946.4 8.5 multiply_bitcast_fusion
  957.7 10.2 reduce-window.76
  969.0 5.1 copy.586
  975.2 6.0 fusion.70
  982.1 9.9 reduce-window.74
  994.4 4.8 copy.582
  999.2 7.2 rev.82
  1006.5 14.1 %add_convert_fusion = (bf16[1024,16,64]{0,2,1:T(8,128)(2,1)}, bf16[1024,16,64]{0,2,1:T(8,128)(2,1)S(1)}) fusion(f32[1024,16,64]{0,2,1:T(8,128)} %bitcast.895, f32[1024,16,64]{0,2,1:T(8,128)} %rev.85, f32[1024,16,64]{0,2,1:T(8,128)} %bitcast.867, f32[1024,16,64]{0,2,1:T(8,128)} %rev.84, f32[1024,16,64]{0,2,1:T(8,128)} %bitcast.894, f32[16]{0:T(128)S(1)} %copy-done.113, ...), kind=kLoop, calls=%fused_computation.127 | loop fusion | flops 10485760 | bytes 37748800 | tf_op jit(solution)/shard_map/convert_element_type | solution.py:207
  1020.6 4.0 copy.438
  (834 shorter events, 596.4 us)
Async XLA Ops:
  7.2 724.1 %all-gather.9.cloned.1.call-start = ((), (), s32[]{:S(2)}) async-start(), calls=%async_computation | async-start | bytes 8912896 | tf_op jit(solution)/shard_map/all_gather | solution.py:19
  8.0 10.9 %copy-start.99 = (f32[16]{0:T(128)}, f32[16]{0:T(128)S(1)}, u32[]{:S(2)}) copy-start(f32[16]{0:T(128)S(1)} %rev.76) | copy-start | bytes 196
  11.4 26.7 %copy-start.46 = (f32[1024,16]{0,1:T(8,128)}, f32[1024,16]{0,1:T(8,128)S(1)}, u32[]{:S(2)}) copy-start(f32[1024,16]{0,1:T(8,128)S(1)} %get-tuple-element.1405) | copy-start | bytes 196612
  11.4 11.1 %copy-start.65 = (f32[4,256,16]{1,0,2:T(4,128)}, f32[4,256,16]{1,0,2:T(4,128)S(1)}, u32[]{:S(2)}) copy-start(f32[4,256,16]{1,0,2:T(4,128)S(1)} %reshape.439) | copy-start | bytes 196612
  15.7 29.5 %copy-start.110 = (f32[16]{0:T(128)}, f32[16]{0:T(128)S(1)}, u32[]{:S(2)}) copy-start(f32[16]{0:T(128)S(1)} %broadcast_multiply_fusion.6) | copy-start | bytes 196
  16.3 28.9 %copy-start.89 = (f32[16]{0:T(128)}, f32[16]{0:T(128)S(1)}, u32[]{:S(2)}) copy-start(f32[16]{0:T(128)S(1)} %get-tuple-element.1393) | copy-start | bytes 196
  16.3 28.9 %copy-start.93 = (f32[16]{0:T(128)}, f32[16]{0:T(128)S(1)}, u32[]{:S(2)}) copy-start(f32[16]{0:T(128)S(1)} %get-tuple-element.1394) | copy-start | bytes 196
  16.3 29.0 %copy-start.95 = (f32[16]{0:T(128)}, f32[16]{0:T(128)S(1)}, u32[]{:S(2)}) copy-start(f32[16]{0:T(128)S(1)} %get-tuple-element.1395) | copy-start | bytes 196
  18.8 33.9 %copy-start.43 = (f32[1024,16]{0,1:T(8,128)}, f32[1024,16]{0,1:T(8,128)S(1)}, u32[]{:S(2)}) copy-start(f32[1024,16]{0,1:T(8,128)S(1)} %rev.75) | copy-start | bytes 196612
  18.8 9.5 copy-start.64
  32.3 10.4 %copy-start.18 = (bf16[1024,128]{1,0:T(8,128)(2,1)S(1)}, bf16[1024,128]{1,0:T(8,128)(2,1)}, u32[]{:S(2)}) copy-start(bf16[1024,128]{1,0:T(8,128)(2,1)} %param.24) | copy-start | bytes 786436
  48.1 683.2 %all-gather.13.cloned.1.call-start = ((), (), s32[]{:S(2)}) async-start(), calls=%async_computation.2 | async-start | bytes 8912896 | tf_op jit(solution)/shard_map/all_gather | solution.py:19
  74.1 657.3 %all-gather.15.cloned.1.call-start = ((), (), s32[]{:S(2)}) async-start(), calls=%async_computation.3 | async-start | bytes 8912896 | tf_op jit(solution)/shard_map/all_gather | solution.py:19
  80.8 650.7 %all-gather.11.cloned.1.call-start = ((), (), s32[]{:S(2)}) async-start(), calls=%async_computation.1 | async-start | bytes 8912896 | tf_op jit(solution)/shard_map/all_gather | solution.py:19
  94.2 10.3 copy-start.112
  94.7 9.8 copy-start.91
  94.7 9.8 copy-start.97
  94.7 9.8 copy-start.98
  100.7 6.7 copy-start.17
  134.3 202.4 %copy-start.20 = (bf16[1024,128]{1,0:T(8,128)(2,1)S(1)}, bf16[1024,128]{1,0:T(8,128)(2,1)}, u32[]{:S(2)}) copy-start(bf16[1024,128]{1,0:T(8,128)(2,1)} %param.23) | copy-start | bytes 786436
  484.9 96.3 %copy-start.12 = (bf16[4,256,16,64]{1,0,3,2:T(4,128)(2,1)S(1)}, bf16[4,256,16,64]{1,0,3,2:T(4,128)(2,1)}, u32[]{:S(2)}) copy-start(bf16[4,256,16,64]{1,0,3,2:T(4,128)(2,1)} %reshape_reshape.11) | copy-start | bytes 6291460
  541.7 47.7 %copy-start.28 = (f32[4,256,256]{2,1,0:T(8,128)S(1)}, f32[4,256,256]{2,1,0:T(8,128)}, u32[]{:S(2)}) copy-start(f32[4,256,256]{2,1,0:T(8,128)} %copy-done.27) | copy-start | bytes 3145732
  581.1 10.2 copy-start.21
  581.1 10.2 copy-start.33
  581.1 10.2 copy-start.34
  581.1 10.2 copy-start.35
  595.1 8.0 copy-start.45
  595.1 8.0 copy-start.81
  792.6 11.5 %copy-start.23 = (f32[16,64,128]{2,1,0:T(8,128)}, f32[16,64,128]{2,1,0:T(8,128)S(1)}, u32[]{:S(2)}) copy-start(f32[16,64,128]{2,1,0:T(8,128)S(1)} %get-tuple-element.1339) | copy-start | bytes 1572868
  792.6 7.6 copy-start.22
  800.2 8.4 copy-start.85
  800.2 8.4 copy-start.109
  800.2 8.4 copy-start.102
  800.2 8.4 copy-start.103
  800.2 8.4 copy-start.104
  800.2 8.4 copy-start.105
  800.2 8.4 copy-start.106
  800.2 8.4 copy-start.107
  800.2 8.4 copy-start.108
  814.7 15.6 %copy-start.4 = (f32[4,256,16,64]{1,3,2,0:T(8,128)S(1)}, f32[4,256,16,64]{1,3,2,0:T(8,128)}, u32[]{:S(2)}) copy-start(f32[4,256,16,64]{1,3,2,0:T(8,128)} %convolution_bitcast_fusion.5) | copy-start | bytes 12582916
  814.7 15.6 %copy-start.6 = (f32[4,256,16,64]{1,0,3,2:T(4,128)S(1)}, f32[4,256,16,64]{1,0,3,2:T(4,128)}, u32[]{:S(2)}) copy-start(f32[4,256,16,64]{1,0,3,2:T(4,128)} %reshape.456) | copy-start | bytes 12582916
  830.3 10.2 copy-start.61
  830.3 10.8 %copy-start.44 = (f32[1024,16]{0,1:T(8,128)S(1)}, f32[1024,16]{0,1:T(8,128)}, u32[]{:S(2)}) copy-start(f32[1024,16]{0,1:T(8,128)} %copy-done.43) | copy-start | bytes 196612
  830.4 10.8 %copy-start.47 = (f32[1024,16]{0,1:T(8,128)S(1)}, f32[1024,16]{0,1:T(8,128)}, u32[]{:S(2)}) copy-start(f32[1024,16]{0,1:T(8,128)} %copy-done.46) | copy-start | bytes 196612
  830.4 50.7 %copy-start.24 = (f32[16,64,128]{2,1,0:T(8,128)S(1)}, f32[16,64,128]{2,1,0:T(8,128)}, u32[]{:S(2)}) copy-start(f32[16,64,128]{2,1,0:T(8,128)} %copy-done.23) | copy-start | bytes 1572868
  879.7 11.7 %copy-start.1 = (f32[16,4,256,64]{2,1,3,0:T(4,128)S(1)}, f32[16,4,256,64]{2,1,3,0:T(4,128)}, u32[]{:S(2)}) copy-start(f32[16,4,256,64]{2,1,3,0:T(4,128)} %get-tuple-element.1991) | copy-start | bytes 12582916
  879.7 11.7 %copy-start.29 = (f32[16,64,128]{2,1,0:T(8,128)S(1)}, f32[16,64,128]{2,1,0:T(8,128)}, u32[]{:S(2)}) copy-start(f32[16,64,128]{2,1,0:T(8,128)} %get-tuple-element.1342) | copy-start | bytes 1572868
  879.7 11.7 %copy-start.32 = (f32[1,16,64,128]{3,2,1,0:T(8,128)S(1)}, f32[1,16,64,128]{3,2,1,0:T(8,128)}, u32[]{:S(2)}) copy-start(f32[1,16,64,128]{3,2,1,0:T(8,128)} %fusion.131) | copy-start | bytes 1572868
  879.7 11.7 %copy-start.49 = (f32[4,256,16]{1,2,0:T(8,128)S(1)}, f32[4,256,16]{1,2,0:T(8,128)}, u32[]{:S(2)}) copy-start(f32[4,256,16]{1,2,0:T(8,128)} %copy-done.48) | copy-start | bytes 196612
  901.3 11.8 %copy-start.56 = (f32[4,256,16]{1,2,0:T(8,128)S(1)}, f32[4,256,16]{1,2,0:T(8,128)}, u32[]{:S(2)}) copy-start(f32[4,256,16]{1,2,0:T(8,128)} %get-tuple-element.1364) | copy-start | bytes 196612
  936.4 7.3 copy-start.63
  936.4 10.0 copy-start.53
  954.9 13.1 %copy-start.60 = (f32[4,16,2,128]{3,1,2,0:T(8,128)S(1)}, f32[4,16,2,128]{3,1,2,0:T(8,128)}, u32[]{:S(2)}) copy-start(f32[4,16,2,128]{3,1,2,0:T(8,128)} %reduce-window.70) | copy-start | bytes 196612
  954.9 13.1 %copy-start.62 = (f32[4,256,16]{1,0,2:T(4,128)S(1)}, f32[4,256,16]{1,0,2:T(4,128)}, u32[]{:S(2)}) copy-start(f32[4,256,16]{1,0,2:T(4,128)} %copy-done.61) | copy-start | bytes 196612
  954.9 13.1 %copy-start.70 = (f32[16,4,256]{2,0,1:T(8,128)S(1)}, f32[16,4,256]{2,0,1:T(8,128)}, u32[]{:S(2)}) copy-start(f32[16,4,256]{2,0,1:T(8,128)} %copy-done.69) | copy-start | bytes 196612
  957.6 16.5 %copy-start.40 = (f32[16,64,128]{2,1,0:T(8,128)S(1)}, f32[16,64,128]{2,1,0:T(8,128)}, u32[]{:S(2)}) copy-start(f32[16,64,128]{2,1,0:T(8,128)} %get-tuple-element.1336) | copy-start | bytes 1572868
  957.6 16.5 %copy-start.42 = (f32[1,16,64,128]{3,2,1,0:T(8,128)S(1)}, f32[1,16,64,128]{3,2,1,0:T(8,128)}, u32[]{:S(2)}) copy-start(f32[1,16,64,128]{3,2,1,0:T(8,128)} %fusion.128) | copy-start | bytes 1572868
  975.2 17.0 %copy-start.58 = (f32[4,256,16]{1,0,2:T(4,128)S(1)}, f32[4,256,16]{1,0,2:T(4,128)}, u32[]{:S(2)}) copy-start(f32[4,256,16]{1,0,2:T(4,128)} %copy-done.57) | copy-start | bytes 196612
  975.2 17.0 %copy-start.59 = (f32[4,16,2,128]{3,1,2,0:T(8,128)S(1)}, f32[4,16,2,128]{3,1,2,0:T(8,128)}, u32[]{:S(2)}) copy-start(f32[4,16,2,128]{3,1,2,0:T(8,128)} %reduce-window.66) | copy-start | bytes 196612
  975.2 17.0 %copy-start.87 = (f32[4,16,2]{1,2,0:T(2,128)S(1)}, f32[4,16,2]{1,2,0:T(2,128)}, u32[]{:S(2)}) copy-start(f32[4,16,2]{1,2,0:T(2,128)} %copy.404) | copy-start | bytes 1540
  975.2 17.0 %copy-start.100 = (f32[16]{0:T(128)S(1)}, f32[16]{0:T(128)}, u32[]{:S(2)}) copy-start(f32[16]{0:T(128)} %copy-done.99) | copy-start | bytes 196
  999.2 7.2 copy-start.113
  1020.6 6.6 copy-start.30
  1020.6 6.6 copy-start.31
  (54 other events, 241.2 us)
Sparse Core Ops, SparseCore 0:
  48.2 77.0 all-gather.8
  127.4 72.8 all-gather.12
  202.5 72.8 all-gather.14
  277.4 72.8 all-gather.10
where the time goes:
time: 1060 us; the launch traced here: 1040 us
  matrix products  436 us (41%)
  local copies, waits for them, and re-layouts  331 us (31%)
  other arithmetic  178 us (17%)
  blocking collectives  74.3 us (7%)
  between operations  15.5 us (1%)
    dot_general x96, matrix products, one_head(): return jnp.einsum('kts,ksp->ktp', weights, value_head, precision=PRECISE)  315 us
    dot_general x10, matrix products, block_parts(): jnp.einsum('ksh,kshp,ksn->khpn', tail_weight, value_blocks, write_blocks,...  58.6 us
    squeeze x64, local copies, waits for them, and re-layouts, emit(): lax.map(jax.checkpoint(one_head), (jnp.transpose(running, (2, 0, 1)), jnp...  54.6 us
    rev x13, local copies, waits for them, and re-layouts, flip_rows(): return jnp.flip(array, 0)  53.7 us
    another operation x17, other arithmetic  53 us
    dynamic_update_slice x128, local copies, waits for them, and re-layouts, emit(): lax.map(jax.checkpoint(one_head), (jnp.transpose(running, (2, 0, 1)), jnp...  46.5 us
    unnamed x8, other arithmetic  44.6 us
    all_gather x2, blocking collectives, entering(): gathered = jax.tree.map(lambda a: lax.all_gather(a, axis), part)  37.7 us
  transfers between devices with their start and end apart: 4, of which 0 were waited for; matrix products, arithmetic and copies ran while one was open for 58% of the time, Pallas kernels for 0%

commit v1 on v0

v1 whole, which is shorter than its diff:
```python
import math

import jax
import jax.numpy as jnp
from jax import lax
from jax.sharding import PartitionSpec as P

SPAN = 128
EXACT = lax.Precision.HIGHEST
HIGH = lax.Precision.HIGH
F32 = jnp.float32


def ein(spec, a, b, precision=HIGH):
    return jnp.einsum(spec, a, b, precision=precision, preferred_element_type=F32)


def scan_over_devices(zone, lams, count, place, reverse):
    sign = -1 if reverse else 1

    def shifted(array, step):
        pairs = [(i, i + sign * step) for i in range(count) if 0 <= i + sign * step < count]
        return lax.ppermute(array, "ctx", pairs)

    state = shifted(zone, 1)
    if count <= 2:
        return state
    logs = lams
    window = 1
    while window < count - 1:
        ids = jnp.arange(count)
        if reverse:
            inside = (ids > place) & (ids <= place + window)
        else:
            inside = (ids < place) & (ids >= place - window)
        weight = jnp.exp(-jnp.sum(jnp.where(inside[:, None, None], logs, 0.0), axis=0))
        state = state + weight[:, :, None] * shifted(state, window)
        window *= 2
    return state


def per_device(
    features, write_map, read_map, step_raw, tokens, base_shift, decay_rate, skip_gain, cotangent
):
    rows, width = features.shape
    heads = decay_rate.shape[0]
    size = width // heads
    span = min(SPAN, rows)
    blocks = rows // span
    count = lax.axis_size("ctx")
    place = lax.axis_index("ctx")
    rates = jnp.concatenate([decay_rate, jnp.flip(decay_rate)])

    codes = jnp.arange(5, dtype=jnp.int32)
    onehot = (tokens[:, None] == codes[None, :]).astype(F32)
    table = jnp.concatenate([base_shift, jnp.flip(base_shift[jnp.array([3, 2, 1, 0, 4])], 1)], 1)
    logits = jnp.concatenate([step_raw, step_raw], 1) + jnp.dot(onehot, table, precision=EXACT)
    steps = jax.nn.softplus(logits)
    slopes = jax.nn.sigmoid(logits)

    fsteps, rsteps = steps[:, :heads], steps[:, heads:]
    drops = (steps * rates[None, :]).reshape(blocks, span, 2 * heads)
    lower = jnp.tril(jnp.ones((span, span), F32))
    upper = lower.T
    strict_lower = lower - jnp.eye(span, dtype=F32)
    strict_upper = strict_lower.T

    def along(tri, array):
        return ein("ts,ksh->kth", tri, array, EXACT)

    rf = along(lower, drops[..., :heads])
    rr = along(upper, drops[..., heads:])
    tot_f, tot_r = rf[:, -1], rr[:, 0]
    ef, er = jnp.exp(-rf), jnp.exp(-rr)
    tf = jnp.exp(rf - tot_f[:, None])
    tr = jnp.exp(rr - tot_r[:, None])
    sf = fsteps.reshape(blocks, span, heads)
    sr = rsteps.reshape(blocks, span, heads)

    expand = (jnp.arange(heads)[:, None] == jnp.arange(width)[None, :] // size).astype(F32)

    def wide(array):
        return jnp.einsum("kth,hw->ktw", array, expand, precision=EXACT)

    def narrow(array):
        return jnp.einsum("ktw,hw->kth", array, expand, precision=HIGH)

    xb = features.reshape(blocks, span, width)
    yb = cotangent.reshape(blocks, span, width)
    bb = write_map.reshape(blocks, span, -1)
    cb = read_map.reshape(blocks, span, -1)
    x32, y32 = xb.astype(F32), yb.astype(F32)
    b32, c32 = bb.astype(F32), cb.astype(F32)

    ef_w, er_w = wide(ef), wide(er)
    xf, xr = wide(tf * sf) * x32, wide(tr * sr) * x32
    yf, yr = ef_w * y32, er_w * y32
    bs_f = ein("ksw,ksn->kwn", xf, b32)
    bs_r = ein("ksw,ksn->kwn", xr, b32)
    ab_f = ein("ktw,ktn->kwn", yf, c32)
    ab_r = ein("ktw,ktn->kwn", yr, c32)

    def columns(array):
        return jnp.repeat(array, size, axis=-1)

    fade_f, fade_r = columns(jnp.exp(-tot_f)), columns(jnp.exp(-tot_r))

    def block_scan(fades, parts, reverse):
        order = range(blocks - 1, -1, -1) if reverse else range(blocks)
        state, weight = jnp.zeros_like(parts[0]), jnp.ones_like(fades[0])
        states, weights = [None] * blocks, [None] * blocks
        for k in order:
            states[k], weights[k] = state, weight
            state = fades[k][:, None] * state + parts[k]
            weight = weight * fades[k]
        return states, weights, state

    sf_loc, sf_wt, zone_f = block_scan(fade_f, bs_f, False)
    sr_loc, sr_wt, zone_r = block_scan(fade_r, bs_r, True)
    af_loc, af_wt, back_f = block_scan(fade_f, ab_f, True)
    ar_loc, ar_wt, back_r = block_scan(fade_r, ab_r, False)

    logs = lax.all_gather(jnp.stack([jnp.sum(tot_f, 0), jnp.sum(tot_r, 0)]), "ctx")
    logs = columns(logs)
    ahead = scan_over_devices(jnp.stack([zone_f, back_r]), logs, count, place, False)
    behind = scan_over_devices(jnp.stack([back_f, zone_r]), logs, count, place, True)

    def entered(local, weights, entry):
        return jnp.stack([s + w[:, None] * entry for s, w in zip(local, weights)])

    state_f = entered(sf_loc, sf_wt, ahead[0])
    state_r = entered(sr_loc, sr_wt, behind[1])
    adj_f = entered(af_loc, af_wt, behind[0])
    adj_r = entered(ar_loc, ar_wt, ahead[1])

    def heads_first(array):
        return jnp.transpose(array.reshape(blocks, span, heads, size), (2, 0, 1, 3))

    xh, yh = heads_first(xb), heads_first(yb)
    turned = lambda array: jnp.transpose(array, (2, 0, 1))
    rf_h, rr_h, sf_h, sr_h = turned(rf), turned(rr), turned(sf), turned(sr)
    t_pos = lax.broadcasted_iota(jnp.int32, (span, span), 0)[None, None]
    s_pos = lax.broadcasted_iota(jnp.int32, (span, span), 1)[None, None]
    spread = jnp.where(
        t_pos >= s_pos,
        rf_h[..., :, None] - rf_h[..., None, :],
        rr_h[..., :, None] - rr_h[..., None, :],
    )
    fade = jnp.exp(-spread)
    size_s = jnp.where(
        t_pos > s_pos,
        sf_h[..., None, :],
        jnp.where(t_pos < s_pos, sr_h[..., None, :], (sf_h + sr_h)[..., None, :]),
    )
    mask = fade * size_s
    scores = ein("ktn,ksn->kts", cb, bb, None)
    weights = mask * scores[None]
    crossed = ein("hktp,hksp->hkts", yh, xh, None)
    d_scores = jnp.sum(crossed * mask, axis=0)
    inner_y = ein("hkts,hksp->hktp", weights, xh.astype(F32))
    inner_x = ein("hkts,hktp->hksp", weights, yh.astype(F32))
    quota = crossed * scores[None] * fade
    pull = quota * size_s
    low, high = t_pos > s_pos, t_pos < s_pos
    back = lambda array: jnp.transpose(array, (1, 2, 0))
    qf = back(jnp.sum(jnp.where(low, quota, 0.0), axis=2))
    qr = back(jnp.sum(jnp.where(high, quota, 0.0), axis=2))
    zf = back(jnp.sum(jnp.where(low, pull, 0.0), axis=3))
    zr = back(jnp.sum(jnp.where(high, pull, 0.0), axis=3))
    flat = lambda array: jnp.transpose(array, (1, 2, 0, 3)).reshape(blocks, span, width)

    both = narrow(x32 * y32)
    center = jnp.sum(c32 * b32, axis=-1)[..., None] * both

    v_f = ein("ktn,kwn->ktw", c32, state_f)
    v_r = ein("ktn,kwn->ktw", c32, state_r)
    u_f = ein("ksn,kwn->ksw", b32, adj_f)
    u_r = ein("ksn,kwn->ksw", b32, adj_r)
    gain = columns(skip_gain + jnp.flip(skip_gain))
    mixed = flat(inner_y) + ef_w * v_f + er_w * v_r + gain * x32
    grad_x = flat(inner_x) + wide(tf * sf) * u_f + wide(tr * sr) * u_r + gain * y32
    grad_c = (
        ein("kts,ksn->ktn", d_scores, b32)
        + ein("ktw,kwn->ktn", yf, state_f)
        + ein("ktw,kwn->ktn", yr, state_r)
    )
    grad_b = (
        ein("kts,ktn->ksn", d_scores, c32)
        + ein("ksw,kwn->ksn", xf, adj_f)
        + ein("ksw,kwn->ksn", xr, adj_r)
    )
    xu_f, xu_r = tf * narrow(x32 * u_f), tr * narrow(x32 * u_r)
    yv_f, yv_r = ef * narrow(y32 * v_f), er * narrow(y32 * v_r)

    def per_head(array):
        return jnp.sum(array.reshape(blocks, heads, -1), axis=-1)

    hold_f = jnp.exp(-tot_f) * per_head(state_f * adj_f)
    hold_r = jnp.exp(-tot_r) * per_head(state_r * adj_r)
    drop_f = (
        along(upper, sf * qf - zf - yv_f) - along(strict_lower, sf * xu_f) - hold_f[:, None]
    )
    drop_r = (
        along(lower, sr * qr - zr - yv_r) - along(strict_upper, sr * xu_r) - hold_r[:, None]
    )
    d_f = (qf + center + xu_f + rates[:heads] * drop_f).reshape(rows, heads)
    d_r = (qr + center + xu_r + rates[heads:] * drop_r).reshape(rows, heads)
    grad_s = d_f * slopes[:, :heads] + d_r * slopes[:, heads:]
    own_gain = jnp.sum(both, axis=(0, 1))
    gains = lax.psum(own_gain + jnp.flip(own_gain), "ctx")
    norm_scale = 1.0 / math.sqrt(rows * count * size)
    return (
        mixed.reshape(rows, width).astype(jnp.bfloat16),
        grad_x.reshape(rows, width).astype(jnp.bfloat16),
        grad_b.reshape(rows, -1).astype(jnp.bfloat16),
        grad_c.reshape(rows, -1).astype(jnp.bfloat16),
        grad_s,
        gains * norm_scale,
    )


def solution(mesh):
    split = P(("groups", "ctx"), None)
    return jax.shard_map(
        per_device,
        mesh=mesh,
        in_specs=(split, split, split, split, P(("groups", "ctx")), P(), P(), P(), split),
        out_specs=(split, split, split, split, split, P("groups")),
        check_vma=False,
    )
```

time: 1060 us -> 614 us (0.58)
  the two profiles are of different devices: /device:TPU:0 before, /device:TPU:28 now
where the time goes in v1:
time: 614 us; the launch traced here: 602 us
  local copies, waits for them, and re-layouts  188 us (31%)
  matrix products  126 us (21%)
  waiting for transfers between devices  115 us (19%)
  other arithmetic  96.8 us (16%)
  blocking collectives  46.4 us (8%)
  starting transfers between devices  27.5 us (4%)
    ppermute x10, waiting for transfers between devices, shifted(): return lax.ppermute(array, 'ctx', pairs)  115 us
    dot_general x24, matrix products, ein(): jnp.einsum(spec, a, b, precision=precision, preferred_element_type=F32)  103 us
    unnamed x361, local copies, waits for them, and re-layouts  65.8 us
    another operation x37, local copies, waits for them, and re-layouts, entered(): return jnp.stack([s + w[:, None] * entry for s, w in zip(local, weights)])  64 us
    unnamed x25, other arithmetic  35.3 us
    psum x1, blocking collectives, per_device(): gains = lax.psum(own_gain + jnp.flip(own_gain), 'ctx')  29.8 us
    ppermute x10, starting transfers between devices, shifted(): return lax.ppermute(array, 'ctx', pairs)  27.5 us
    all_gather x1, blocking collectives, per_device(): lax.all_gather(jnp.stack([jnp.sum(tot_f, 0), jnp.sum(tot_r, 0)]), 'ctx')  16.6 us
  transfers between devices with their start and end apart: 10, of which 7 were waited for; matrix products, arithmetic and copies ran while one was open for 30% of the time, Pallas kernels for 0%

profile of v1, /device:TPU:28, one launch (start us, length us, event | category | flops | bytes accessed | tf_op | source)
XLA Modules:
  0.0 602.1 jit_solution(6057230228814341870)
XLA Ops:
  4.1 2.2 add_divide_fusion
  24.3 2.4 fusion.49
  27.5 2.6 slice_add_fusion
  30.2 2.4 fusion.53
  33.4 2.8 slice_add_fusion.1
  37.3 2.1 collective-permute-start.5
  42.4 3.9 copy.194
  46.3 2.6 copy.210
  48.9 3.1 fusion.163
  52.2 16.6 %all-gather.1 = f32[16,2,16]{2,1,0:T(2,128)S(1)} all-gather(f32[1,2,16]{2,1,0:T(2,128)S(1)} %maximum_bitcast_fusion), channel_id=2, replica_groups=mesh['groups'=2,'ctx'=16] {'ctx'}, dimensions={0}, use_global_device_ids=true | all-gather | bytes 2176 | tf_op jit(solution)/shard_map/all_gather | solution.py:123
  75.0 3.5 copy.251
  78.6 3.5 copy.252
  82.2 29.8 %psum.7 = f32[16]{0:T(128)} all-reduce(f32[16]{0:T(128)S(1)} %add.568), channel_id=1, replica_groups=mesh['groups'=2,'ctx'=16] {'ctx'}, use_global_device_ids=true, to_apply=%region_19.20 | all-reduce | flops 16 | bytes 128 | tf_op jit(solution)/shard_map/psum | solution.py:210
  112.0 15.5 %select_reduce_fusion.2 = (f32[16,8,128]{2,1,0:T(8,128)S(1)}, f32[16,8,128]{2,1,0:T(8,128)S(1)}, f32[16,8,128]{2,1,0:T(8,128)S(1)}, f32[16,8,128]{2,1,0:T(8,128)}, f32[8,128,128]{2,1,0:T(8,128)S(1)}) fusion(f32[16,8,128]{2,1,0:T(8,128)} %bitcast_add_fusion.4, f32[16,8,128]{2,1,0:T(8,128)S(1)} %bitcast.300, f32[16,8,128]{2,1,0:T(8,128)S(1)} %bitcast.303, ...), kind=kOutput, calls=%fused_computation.14 | convolution fusion | flops 310181888 | bytes 5881856 | tf_op jit(solution)/shard_map/hktp,hksp->hkts/dot_general | solution.py:15
  127.5 2.0 collective-permute-start.6
  132.0 3.8 fusion.85
  135.8 6.4 %collective-permute-done.6 = f32[2,1024,128]{2,1,0:T(8,128)S(1)} collective-permute-done((f32[2,1024,128]{2,1,0:T(8,128)}, f32[2,1024,128]{2,1,0:T(8,128)S(1)}, u32[]{:S(2)}, u32[]{:S(2)}) %collective-permute-start.6) | collective-permute-done | bytes 1048608 | tf_op jit(solution)/shard_map/ppermute | solution.py:23
  145.8 8.4 %fusion.57 = f32[8,128,16,64]{1,3,0,2:T(8,128)} fusion(f32[8,128,128]{2,1,0:T(8,128)S(1)} %copy-done.68, f32[16,8,128]{2,1,0:T(8,128)S(1)} %copy-done.97, f32[16,8,128]{2,1,0:T(8,128)S(1)} %bitcast.301, f32[16,8,128]{2,1,0:T(8,128)S(1)} %bitcast.304, f32[16,8,128]{2,1,0:T(8,128)S(1)} %copy-done.102, f32[16,8,128]{2,1,0:T(8,128)S(1)} %copy-done.101, ...), kind=kOutput, calls=%fused_computation.79 | convolution fusion | flops 822083584 | bytes 7192576 | tf_op jit(solution)/shard_map/hkts,hktp->hksp/dot_general | solution.py:15
  154.2 12.5 %collective-permute-done.7 = f32[2,1024,128]{2,1,0:T(8,128)S(1)} collective-permute-done((f32[2,1024,128]{2,1,0:T(8,128)S(1)}, f32[2,1024,128]{2,1,0:T(8,128)S(1)}, u32[]{:S(2)}, u32[]{:S(2)}) %collective-permute-start.7) | collective-permute-done | bytes 1048608 | tf_op jit(solution)/shard_map/ppermute | solution.py:23
  169.4 10.0 %fusion.54 = f32[8,128,16,64]{1,3,0,2:T(8,128)} fusion(f32[8,128,128]{2,1,0:T(8,128)S(1)} %copy-done.68, f32[16,8,128]{2,1,0:T(8,128)S(1)} %copy-done.97, f32[16,8,128]{2,1,0:T(8,128)S(1)} %bitcast.302, f32[16,8,128]{2,1,0:T(8,128)S(1)} %bitcast.305, f32[16,8,128]{2,1,0:T(8,128)S(1)} %copy-done.102, f32[16,8,128]{2,1,0:T(8,128)S(1)} %copy-done.101, ...), kind=kOutput, calls=%fused_computation.78 | convolution fusion | flops 822083584 | bytes 7192576 | tf_op jit(solution)/shard_map/hkts,hksp->hktp/dot_general | solution.py:15
  179.4 11.3 %collective-permute-done.8 = f32[2,1024,128]{2,1,0:T(8,128)S(1)} collective-permute-done((f32[2,1024,128]{2,1,0:T(8,128)S(1)}, f32[2,1024,128]{2,1,0:T(8,128)S(1)}, u32[]{:S(2)}, u32[]{:S(2)}) %collective-permute-start.8) | collective-permute-done | bytes 1048608 | tf_op jit(solution)/shard_map/ppermute | solution.py:23
  191.9 12.4 %collective-permute-start.9 = (f32[2,1024,128]{2,1,0:T(8,128)}, f32[2,1024,128]{2,1,0:T(8,128)}, u32[]{:S(2)}, u32[]{:S(2)}) collective-permute-start(f32[2,1024,128]{2,1,0:T(8,128)} %multiply_add_fusion.1), channel_id=1, source_target_pairs={{8,0},{9,1},{10,2},{11,3},{12,4},{13,5},{14,6},{15,7},{24,16},{25,... | collective-permute-start | bytes 3145736 | tf_op jit(solution)/shard_map/ppermute | solution.py:23
  210.3 4.7 copy.196
  215.0 5.4 copy.205
  220.3 4.7 copy.212
  225.0 5.4 copy.213
  238.4 4.6 fusion.51
  243.1 3.0 slice_add_fusion.16
  246.2 2.5 multiply_add_fusion
  256.5 2.7 constant_dynamic-update-slice_fusion.15
  261.3 2.0 copy-done.11
  265.6 2.4 fusion.97
  269.9 2.4 fusion.47
  272.4 2.8 slice_add_fusion.24
  276.3 2.1 collective-permute-start
  285.4 2.6 constant_dynamic-update-slice_fusion.13
  289.9 2.3 constant_dynamic-update-slice_fusion.12
  294.2 2.5 constant_dynamic-update-slice_fusion.11
  298.6 2.2 constant_dynamic-update-slice_fusion.10
  329.4 6.8 %collective-permute-done.1 = f32[2,1024,128]{2,1,0:T(8,128)} collective-permute-done((f32[2,1024,128]{2,1,0:T(8,128)}, f32[2,1024,128]{2,1,0:T(8,128)}, u32[]{:S(2)}, u32[]{:S(2)}) %collective-permute-start.1) | collective-permute-done | bytes 1048608 | tf_op jit(solution)/shard_map/ppermute | solution.py:23
  336.2 2.9 multiply_add_fusion.7
  343.1 2.0 constant_dynamic-update-slice_fusion.42
  345.2 19.1 %collective-permute-done.2 = f32[2,1024,128]{2,1,0:T(8,128)} collective-permute-done((f32[2,1024,128]{2,1,0:T(8,128)}, f32[2,1024,128]{2,1,0:T(8,128)}, u32[]{:S(2)}, u32[]{:S(2)}) %collective-permute-start.2) | collective-permute-done | bytes 1048608 | tf_op jit(solution)/shard_map/ppermute | solution.py:23
  364.3 2.8 multiply_add_fusion.6
  368.4 6.6 %fusion.68 = f32[8,128,128]{2,1,0:T(8,128)} fusion(f32[8,128,128]{2,1,0:T(8,128)S(1)} %copy-done.48, f32[8,1024,128]{2,1,0:T(8,128)} %copy-done.22, f32[8,128,1024]{2,1,0:T(8,128)} %copy-done.10, bf16[8,128,1024]{2,1,0:T(8,128)(2,1)S(1)} %bitcast.269), kind=kOutput, calls=%fused_computation.88 | convolution fusion | flops 807534592 | bytes 11534336 | tf_op jit(solution)/shard_map/ksw,kwn->ksn/dot_general | solution.py:15
  382.9 9.5 %collective-permute-done.3 = f32[2,1024,128]{2,1,0:T(8,128)} collective-permute-done((f32[2,1024,128]{2,1,0:T(8,128)}, f32[2,1024,128]{2,1,0:T(8,128)}, u32[]{:S(2)}, u32[]{:S(2)}) %collective-permute-start.3) | collective-permute-done | bytes 1048608 | tf_op jit(solution)/shard_map/ppermute | solution.py:23
  392.3 2.8 multiply_add_fusion.5
  398.5 2.0 constant_dynamic-update-slice_fusion.40
  400.5 49.2 %collective-permute-done.4 = f32[2,1024,128]{2,1,0:T(8,128)} collective-permute-done((f32[2,1024,128]{2,1,0:T(8,128)}, f32[2,1024,128]{2,1,0:T(8,128)}, u32[]{:S(2)}, u32[]{:S(2)}) %collective-permute-start.4) | collective-permute-done | bytes 1048608 | tf_op jit(solution)/shard_map/ppermute | solution.py:23
  456.1 3.3 constant_dynamic-update-slice_fusion.9
  472.0 4.2 fusion.168
  478.8 19.8 %fusion.12 = (bf16[8,128,1024]{2,1,0:T(8,128)(2,1)}, bf16[8,128,1024]{2,1,0:T(8,128)(2,1)}, f32[8,1024,128]{1,2,0:T(8,128)}) fusion(bf16[8,128,1024]{2,1,0:T(8,128)(2,1)S(1)} %bitcast.260, f32[8,128,1024]{2,1,0:T(8,128)} %copy-done.6, f32[8,128,1024]{2,1,0:T(8,128)} %copy.213, f32[8,128,1024]{2,1,0:T(8,128)} %copy-done.10, f32[8,1024,128]{1,2,0:T(8,128)} %copy-done.11, ...), kind=kOutput, calls=%fused_computation.30 | convolution fusion | flops 822083584 | bytes 54792192 | tf_op jit(solution)/shard_map/ksn,kwn->ksw/dot_general | solution.py:15
  498.6 4.2 fusion.10
  504.9 2.5 fusion.96
  521.0 2.0 stack.171
  529.8 2.0 constant_dynamic-update-slice_fusion.62
  542.2 2.8 multiply_reduce_fusion.1
  545.0 2.0 stack.140
  562.4 2.5 constant_dynamic-update-slice_fusion.37
  572.2 2.9 multiply_reduce_fusion.2
  579.8 3.7 bitcast_add_fusion.2
  586.0 6.0 %fusion.65 = f32[8,128,128]{2,1,0:T(8,128)S(1)} fusion(f32[8,128,128]{2,1,0:T(8,128)} %fusion.171, f32[8,1024,128]{2,1,0:T(8,128)} %copy-done.21, f32[8,128,1024]{2,1,0:T(8,128)} %copy-done.8, bf16[8,128,1024]{2,1,0:T(8,128)(2,1)S(1)} %bitcast.261), kind=kOutput, calls=%fused_computation.85 | convolution fusion | flops 807534592 | bytes 11534336 | tf_op jit(solution)/shard_map/ktw,kwn->ktn/dot_general | solution.py:15
  592.1 5.7 fusion.70
  597.8 3.4 fusion.69
  (551 shorter events, 214.4 us)
Async XLA Ops:
  6.8 13.7 %copy-start.30 = (f32[8,16,128]{1,0,2:T(8,128)}, f32[8,16,128]{1,0,2:T(8,128)S(1)}, u32[]{:S(2)}) copy-start(f32[8,16,128]{1,0,2:T(8,128)S(1)} %copy.202) | copy-start | bytes 196612
  7.4 13.1 %copy-start.107 = (f32[8,16]{1,0:T(8,128)}, f32[8,16]{1,0:T(8,128)S(1)}, u32[]{:S(2)}) copy-start(f32[8,16]{1,0:T(8,128)S(1)} %get-tuple-element.134) | copy-start | bytes 1540
  14.7 24.7 %copy-start.25 = (f32[8,16,128]{1,0,2:T(8,128)}, f32[8,16,128]{1,0,2:T(8,128)S(1)}, u32[]{:S(2)}) copy-start(f32[8,16,128]{1,0,2:T(8,128)S(1)} %copy.197) | copy-start | bytes 196612
  37.3 90.2 %collective-permute-start.5 = (f32[2,1024,128]{2,1,0:T(8,128)}, f32[2,1024,128]{2,1,0:T(8,128)}, u32[]{:S(2)}, u32[]{:S(2)}) collective-permute-start(f32[2,1024,128]{2,1,0:T(8,128)} %pad_maximum_fusion.1), channel_id=1, source_target_pairs={{1,0},{2,1},{3,2},{4,3},{5,4},{6,5},{7,6},{8,7},{9,8},{10,9},{11,1... | collective-permute-start | bytes 3145736 | tf_op jit(solution)/shard_map/ppermute | solution.py:23
  46.3 26.1 %copy-start.70 = (f32[2,8,8,128]{3,1,2,0:T(8,128)S(1)}, f32[2,8,8,128]{3,1,2,0:T(8,128)}, u32[]{:S(2)}) copy-start(f32[2,8,8,128]{3,1,2,0:T(8,128)} %get-tuple-element.140) | copy-start | bytes 196612
  46.3 27.3 %copy-start.67 = (f32[8,16,128]{2,1,0:T(8,128)S(1)}, f32[8,16,128]{2,1,0:T(8,128)}, u32[]{:S(2)}) copy-start(f32[8,16,128]{2,1,0:T(8,128)} %copy-done.66) | copy-start | bytes 196612
  112.0 17.6 %copy-start.100 = (f32[2,16,64]{2,1,0:T(8,128)S(1)}, f32[2,16,64]{2,1,0:T(8,128)}, u32[]{:S(2)}) copy-start(f32[2,16,64]{2,1,0:T(8,128)} %get-tuple-element.12) | copy-start | bytes 24580
  112.0 18.2 %copy-start.99 = (f32[2,16,64]{2,1,0:T(8,128)S(1)}, f32[2,16,64]{2,1,0:T(8,128)}, u32[]{:S(2)}) copy-start(f32[2,16,64]{2,1,0:T(8,128)} %get-tuple-element.13) | copy-start | bytes 24580
  112.0 20.0 %copy-start.65 = (f32[8,128,16]{2,0,1:T(8,128)S(1)}, f32[8,128,16]{2,0,1:T(8,128)}, u32[]{:S(2)}) copy-start(f32[8,128,16]{2,0,1:T(8,128)} %get-tuple-element.136) | copy-start | bytes 196612
  127.5 14.7 %copy-start.125 = (f32[2,1024]{1,0:T(2,128)S(1)}, f32[2,1024]{1,0:T(2,128)}, u32[]{:S(2)}) copy-start(f32[2,1024]{1,0:T(2,128)} %exp.133) | copy-start | bytes 24580
  127.5 14.7 %collective-permute-start.6 = (f32[2,1024,128]{2,1,0:T(8,128)}, f32[2,1024,128]{2,1,0:T(8,128)S(1)}, u32[]{:S(2)}, u32[]{:S(2)}) collective-permute-start(f32[2,1024,128]{2,1,0:T(8,128)} %collective-permute-done.5), channel_id=1, source_target_pairs={{1,0},{2,1},{3,2},{4,3},{5,4},{6,5},{7,6},{8,7},{9,8},{10,9},{11,1... | collective-permute-start | bytes 3145736 | tf_op jit(solution)/shard_map/ppermute | solution.py:23
  131.9 13.2 %copy-start.98 = (f32[2,16,64]{2,1,0:T(8,128)S(1)}, f32[2,16,64]{2,1,0:T(8,128)}, u32[]{:S(2)}) copy-start(f32[2,16,64]{2,1,0:T(8,128)} %get-tuple-element.11) | copy-start | bytes 24580
  131.9 13.8 %copy-start.54 = (bf16[128,8,8,128]{3,2,1,0:T(8,128)(2,1)S(1)}, bf16[128,8,8,128]{3,2,1,0:T(8,128)(2,1)}, u32[]{:S(2)}) copy-start(bf16[128,8,8,128]{3,2,1,0:T(8,128)(2,1)} %copy.252) | copy-start | bytes 6291460
  131.9 13.8 %copy-start.68 = (f32[8,128,128]{2,1,0:T(8,128)S(1)}, f32[8,128,128]{2,1,0:T(8,128)}, u32[]{:S(2)}) copy-start(f32[8,128,128]{2,1,0:T(8,128)} %fusion.166) | copy-start | bytes 1572868
  131.9 13.8 %copy-start.97 = (f32[16,8,128]{2,1,0:T(8,128)S(1)}, f32[16,8,128]{2,1,0:T(8,128)}, u32[]{:S(2)}) copy-start(f32[16,8,128]{2,1,0:T(8,128)} %bitcast_add_fusion.4) | copy-start | bytes 196612
  131.9 13.8 %copy-start.101 = (f32[16,8,128]{2,1,0:T(8,128)S(1)}, f32[16,8,128]{2,1,0:T(8,128)}, u32[]{:S(2)}) copy-start(f32[16,8,128]{2,1,0:T(8,128)} %copy.189) | copy-start | bytes 196612
  131.9 13.8 %copy-start.102 = (f32[16,8,128]{2,1,0:T(8,128)S(1)}, f32[16,8,128]{2,1,0:T(8,128)}, u32[]{:S(2)}) copy-start(f32[16,8,128]{2,1,0:T(8,128)} %copy.192) | copy-start | bytes 196612
  131.9 13.8 %copy-start.152 = (pred[128,128]{1,0:T(8,128)(4,1)S(1)}, pred[128,128]{1,0:T(8,128)(4,1)}, u32[]{:S(2)}) copy-start(pred[128,128]{1,0:T(8,128)(4,1)} %get-tuple-element.181) | copy-start | bytes 49156
  131.9 13.8 %copy-start.153 = (pred[128,128]{1,0:T(8,128)(4,1)S(1)}, pred[128,128]{1,0:T(8,128)(4,1)}, u32[]{:S(2)}) copy-start(pred[128,128]{1,0:T(8,128)(4,1)} %get-tuple-element.182) | copy-start | bytes 49156
  132.0 13.8 %copy-start.154 = (pred[128,128]{1,0:T(8,128)(4,1)S(1)}, pred[128,128]{1,0:T(8,128)(4,1)}, u32[]{:S(2)}) copy-start(pred[128,128]{1,0:T(8,128)(4,1)} %iota_compare_fusion.6) | copy-start | bytes 49156
  143.7 23.0 %collective-permute-start.7 = (f32[2,1024,128]{2,1,0:T(8,128)S(1)}, f32[2,1024,128]{2,1,0:T(8,128)S(1)}, u32[]{:S(2)}, u32[]{:S(2)}) collective-permute-start(f32[2,1024,128]{2,1,0:T(8,128)S(1)} %multiply_add_fusion.3), channel_id=1, source_target_pairs={{2,0},{3,1},{4,2},{5,3},{6,4},{7,5},{8,6},{9,7},{10,8},{11,9},{12,... | collective-permute-start | bytes 3145736 | tf_op jit(solution)/shard_map/ppermute | solution.py:23
  145.8 21.0 %copy-start.124 = (f32[2,1024]{1,0:T(2,128)S(1)}, f32[2,1024]{1,0:T(2,128)}, u32[]{:S(2)}) copy-start(f32[2,1024]{1,0:T(2,128)} %exp.135) | copy-start | bytes 24580
  145.8 23.1 %copy-start.161 = (f32[16]{0:T(128)S(1)}, f32[16]{0:T(128)}, u32[]{:S(2)}) copy-start(f32[16]{0:T(128)} %psum.7) | copy-start | bytes 196
  145.8 23.6 %copy-start.53 = (bf16[128,8,8,128]{3,2,1,0:T(8,128)(2,1)S(1)}, bf16[128,8,8,128]{3,2,1,0:T(8,128)(2,1)}, u32[]{:S(2)}) copy-start(bf16[128,8,8,128]{3,2,1,0:T(8,128)(2,1)} %copy.251) | copy-start | bytes 6291460
  167.1 23.6 %collective-permute-start.8 = (f32[2,1024,128]{2,1,0:T(8,128)S(1)}, f32[2,1024,128]{2,1,0:T(8,128)S(1)}, u32[]{:S(2)}, u32[]{:S(2)}) collective-permute-start(f32[2,1024,128]{2,1,0:T(8,128)S(1)} %multiply_add_fusion.2), channel_id=1, source_target_pairs={{4,0},{5,1},{6,2},{7,3},{8,4},{9,5},{10,6},{11,7},{12,8},{13,9},{1... | collective-permute-start | bytes 3145736 | tf_op jit(solution)/shard_map/ppermute | solution.py:23
  169.4 21.3 %copy-start.123 = (f32[2,1024]{1,0:T(2,128)S(1)}, f32[2,1024]{1,0:T(2,128)}, u32[]{:S(2)}) copy-start(f32[2,1024]{1,0:T(2,128)} %exp.137) | copy-start | bytes 24580
  179.4 28.2 %copy-start.103 = (f32[2,16,64]{2,1,0:T(8,128)S(1)}, f32[2,16,64]{2,1,0:T(8,128)}, u32[]{:S(2)}) copy-start(f32[2,16,64]{2,1,0:T(8,128)} %negate_exponential_fusion.10) | copy-start | bytes 24580
  179.4 28.9 %copy-start.104 = (f32[2,16,64]{2,1,0:T(8,128)S(1)}, f32[2,16,64]{2,1,0:T(8,128)}, u32[]{:S(2)}) copy-start(f32[2,16,64]{2,1,0:T(8,128)} %negate_exponential_fusion.9) | copy-start | bytes 24580
  179.4 29.5 %copy-start.105 = (f32[2,16,64]{2,1,0:T(8,128)S(1)}, f32[2,16,64]{2,1,0:T(8,128)}, u32[]{:S(2)}) copy-start(f32[2,16,64]{2,1,0:T(8,128)} %negate_exponential_fusion.8) | copy-start | bytes 24580
  179.4 30.2 %copy-start.106 = (f32[2,16,64]{2,1,0:T(8,128)S(1)}, f32[2,16,64]{2,1,0:T(8,128)}, u32[]{:S(2)}) copy-start(f32[2,16,64]{2,1,0:T(8,128)} %negate_exponential_fusion.7) | copy-start | bytes 24580
  191.9 54.2 %collective-permute-start.9 = (f32[2,1024,128]{2,1,0:T(8,128)}, f32[2,1024,128]{2,1,0:T(8,128)}, u32[]{:S(2)}, u32[]{:S(2)}) collective-permute-start(f32[2,1024,128]{2,1,0:T(8,128)} %multiply_add_fusion.1), channel_id=1, source_target_pairs={{8,0},{9,1},{10,2},{11,3},{12,4},{13,5},{14,6},{15,7},{24,16},{25,... | collective-permute-start | bytes 3145736 | tf_op jit(solution)/shard_map/ppermute | solution.py:23
  225.0 11.3 %copy-start.151 = (f32[1024]{0:T(1024)S(1)}, f32[1024]{0:T(1024)}, u32[]{:S(2)}) copy-start(f32[1024]{0:T(1024)} %multiply_reduce_fusion.3) | copy-start | bytes 12292
  275.1 10.3 %copy-start.142 = (f32[1024]{0:T(1024)S(1)}, f32[1024]{0:T(1024)}, u32[]{:S(2)}) copy-start(f32[1024]{0:T(1024)} %get-tuple-element.152) | copy-start | bytes 12292
  276.3 43.5 %collective-permute-start = (f32[2,1024,128]{2,1,0:T(8,128)}, f32[2,1024,128]{2,1,0:T(8,128)}, u32[]{:S(2)}, u32[]{:S(2)}) collective-permute-start(f32[2,1024,128]{2,1,0:T(8,128)} %pad_maximum_fusion), channel_id=1, source_target_pairs={{0,1},{1,2},{2,3},{3,4},{4,5},{5,6},{6,7},{7,8},{8,9},{9,10},{10,1... | collective-permute-start | bytes 3145736 | tf_op jit(solution)/shard_map/ppermute | solution.py:23
  278.4 11.5 %copy-start.141 = (f32[1024]{0:T(1024)S(1)}, f32[1024]{0:T(1024)}, u32[]{:S(2)}) copy-start(f32[1024]{0:T(1024)} %get-tuple-element.153) | copy-start | bytes 12292
  283.5 10.7 %copy-start.139 = (f32[1024]{0:T(1024)S(1)}, f32[1024]{0:T(1024)}, u32[]{:S(2)}) copy-start(f32[1024]{0:T(1024)} %get-tuple-element.154) | copy-start | bytes 12292
  288.0 10.7 %copy-start.138 = (f32[1024]{0:T(1024)S(1)}, f32[1024]{0:T(1024)}, u32[]{:S(2)}) copy-start(f32[1024]{0:T(1024)} %get-tuple-element.155) | copy-start | bytes 12292
  304.7 8.5 %copy-start.63 = (f32[1,16,8192]{2,1,0:T(8,128)S(1)}, f32[1,16,8192]{2,1,0:T(8,128)}, u32[]{:S(2)}) copy-start(f32[1,16,8192]{2,1,0:T(8,128)} %stack.163) | copy-start | bytes 1572868
  313.2 23.0 %copy-start.122 = (f32[2,1024]{1,0:T(2,128)S(1)}, f32[2,1024]{1,0:T(2,128)}, u32[]{:S(2)}) copy-start(f32[2,1024]{1,0:T(2,128)} %exp.124) | copy-start | bytes 24580
  319.8 16.4 %collective-permute-start.1 = (f32[2,1024,128]{2,1,0:T(8,128)}, f32[2,1024,128]{2,1,0:T(8,128)}, u32[]{:S(2)}, u32[]{:S(2)}) collective-permute-start(f32[2,1024,128]{2,1,0:T(8,128)} %collective-permute-done), channel_id=1, source_target_pairs={{0,1},{1,2},{2,3},{3,4},{4,5},{5,6},{6,7},{7,8},{8,9},{9,10},{10,1... | collective-permute-start | bytes 3145736 | tf_op jit(solution)/shard_map/ppermute | solution.py:23
  325.5 38.7 %copy-start.121 = (f32[2,1024]{1,0:T(2,128)S(1)}, f32[2,1024]{1,0:T(2,128)}, u32[]{:S(2)}) copy-start(f32[2,1024]{1,0:T(2,128)} %exp.126) | copy-start | bytes 24580
  327.5 12.9 %copy-start.64 = (f32[1,16,8192]{2,1,0:T(8,128)S(1)}, f32[1,16,8192]{2,1,0:T(8,128)}, u32[]{:S(2)}) copy-start(f32[1,16,8192]{2,1,0:T(8,128)} %stack.153) | copy-start | bytes 1572868
  339.1 25.2 %collective-permute-start.2 = (f32[2,1024,128]{2,1,0:T(8,128)}, f32[2,1024,128]{2,1,0:T(8,128)}, u32[]{:S(2)}, u32[]{:S(2)}) collective-permute-start(f32[2,1024,128]{2,1,0:T(8,128)} %multiply_add_fusion.7), channel_id=1, source_target_pairs={{0,2},{1,3},{2,4},{3,5},{4,6},{5,7},{6,8},{7,9},{8,10},{9,11},{10,... | collective-permute-start | bytes 3145736 | tf_op jit(solution)/shard_map/ppermute | solution.py:23
  343.1 25.3 %copy-start.4 = (bf16[1024,1024]{1,0:T(8,128)(2,1)S(1)}, bf16[1024,1024]{1,0:T(8,128)(2,1)}, u32[]{:S(2)}) copy-start(bf16[1024,1024]{1,0:T(8,128)(2,1)} %param.10) | copy-start | bytes 6291460
  343.1 25.3 %copy-start.48 = (f32[8,128,128]{2,1,0:T(8,128)S(1)}, f32[8,128,128]{2,1,0:T(8,128)}, u32[]{:S(2)}) copy-start(f32[8,128,128]{2,1,0:T(8,128)} %fusion.170) | copy-start | bytes 1572868
  367.1 25.2 %collective-permute-start.3 = (f32[2,1024,128]{2,1,0:T(8,128)}, f32[2,1024,128]{2,1,0:T(8,128)}, u32[]{:S(2)}, u32[]{:S(2)}) collective-permute-start(f32[2,1024,128]{2,1,0:T(8,128)} %multiply_add_fusion.6), channel_id=1, source_target_pairs={{0,4},{1,5},{2,6},{3,7},{4,8},{5,9},{6,10},{7,11},{8,12},{9,13},{1... | collective-permute-start | bytes 3145736 | tf_op jit(solution)/shard_map/ppermute | solution.py:23
  375.0 17.3 %copy-start.120 = (f32[2,1024]{1,0:T(2,128)S(1)}, f32[2,1024]{1,0:T(2,128)}, u32[]{:S(2)}) copy-start(f32[2,1024]{1,0:T(2,128)} %exp.128) | copy-start | bytes 24580
  377.0 72.7 %copy-start.119 = (f32[2,1024]{1,0:T(2,128)S(1)}, f32[2,1024]{1,0:T(2,128)}, u32[]{:S(2)}) copy-start(f32[2,1024]{1,0:T(2,128)} %exp.130) | copy-start | bytes 24580
  380.9 15.6 %copy-start.49 = (f32[8,128,16]{2,0,1:T(8,128)S(1)}, f32[8,128,16]{2,0,1:T(8,128)}, u32[]{:S(2)}) copy-start(f32[8,128,16]{2,0,1:T(8,128)} %get-tuple-element.115) | copy-start | bytes 196612
  382.9 68.8 %copy-start.93 = (f32[1024]{0:T(1024)S(1)}, f32[1024]{0:T(1024)}, u32[]{:S(2)}) copy-start(f32[1024]{0:T(1024)} %broadcast_in_dim.315) | copy-start | bytes 12292
  395.2 54.6 %collective-permute-start.4 = (f32[2,1024,128]{2,1,0:T(8,128)}, f32[2,1024,128]{2,1,0:T(8,128)}, u32[]{:S(2)}, u32[]{:S(2)}) collective-permute-start(f32[2,1024,128]{2,1,0:T(8,128)} %multiply_add_fusion.5), channel_id=1, source_target_pairs={{0,8},{1,9},{2,10},{3,11},{4,12},{5,13},{6,14},{7,15},{16,24},{17,... | collective-permute-start | bytes 3145736 | tf_op jit(solution)/shard_map/ppermute | solution.py:23
  396.5 56.4 %copy-start.137 = (f32[1024]{0:T(1024)S(1)}, f32[1024]{0:T(1024)}, u32[]{:S(2)}) copy-start(f32[1024]{0:T(1024)} %get-tuple-element.46) | copy-start | bytes 12292
  398.5 53.2 %copy-start.20 = (f32[8,1024,128]{2,1,0:T(8,128)S(1)}, f32[8,1024,128]{2,1,0:T(8,128)}, u32[]{:S(2)}) copy-start(f32[8,1024,128]{2,1,0:T(8,128)} %copy-done.19) | copy-start | bytes 12582916
  398.5 54.4 %copy-start.40 = (f32[1,1024,128]{2,1,0:T(8,128)S(1)}, f32[1,1024,128]{2,1,0:T(8,128)}, u32[]{:S(2)}) copy-start(f32[1,1024,128]{2,1,0:T(8,128)} %get-tuple-element.86) | copy-start | bytes 1572868
  400.5 53.4 %copy-start.136 = (f32[1024]{0:T(1024)S(1)}, f32[1024]{0:T(1024)}, u32[]{:S(2)}) copy-start(f32[1024]{0:T(1024)} %get-tuple-element.45) | copy-start | bytes 12292
  507.4 12.7 %copy-start.51 = (f32[1,1024,128]{2,1,0:T(8,128)S(1)}, f32[1,1024,128]{2,1,0:T(8,128)}, u32[]{:S(2)}) copy-start(f32[1,1024,128]{2,1,0:T(8,128)} %get-tuple-element.54) | copy-start | bytes 1572868
  521.0 7.9 %copy-start.52 = (f32[1,1024,128]{2,1,0:T(8,128)S(1)}, f32[1,1024,128]{2,1,0:T(8,128)}, u32[]{:S(2)}) copy-start(f32[1,1024,128]{2,1,0:T(8,128)} %get-tuple-element.88) | copy-start | bytes 1572868
  529.8 11.5 %copy-start.59 = (f32[1,16,8192]{2,1,0:T(8,128)S(1)}, f32[1,16,8192]{2,1,0:T(8,128)}, u32[]{:S(2)}) copy-start(f32[1,16,8192]{2,1,0:T(8,128)} %stack.174) | copy-start | bytes 1572868
  529.8 12.3 %copy-start.32 = (f32[8,16,8192]{2,1,0:T(8,128)S(1)}, f32[8,16,8192]{2,1,0:T(8,128)}, u32[]{:S(2)}) copy-start(f32[8,16,8192]{2,1,0:T(8,128)} %constant_dynamic-update-slice_fusion.50) | copy-start | bytes 12582916
  529.8 12.3 %copy-start.58 = (f32[1,16,8192]{2,1,0:T(8,128)S(1)}, f32[1,16,8192]{2,1,0:T(8,128)}, u32[]{:S(2)}) copy-start(f32[1,16,8192]{2,1,0:T(8,128)} %stack.164) | copy-start | bytes 1572868
  529.8 12.4 %copy-start.55 = (f32[1,16,8192]{2,1,0:T(8,128)S(1)}, f32[1,16,8192]{2,1,0:T(8,128)}, u32[]{:S(2)}) copy-start(f32[1,16,8192]{2,1,0:T(8,128)} %stack.165) | copy-start | bytes 1572868
  561.6 8.9 %copy-start.61 = (f32[1,16,8192]{2,1,0:T(8,128)S(1)}, f32[1,16,8192]{2,1,0:T(8,128)}, u32[]{:S(2)}) copy-start(f32[1,16,8192]{2,1,0:T(8,128)} %stack.146) | copy-start | bytes 1572868
  561.6 9.8 %copy-start.62 = (f32[1,16,8192]{2,1,0:T(8,128)S(1)}, f32[1,16,8192]{2,1,0:T(8,128)}, u32[]{:S(2)}) copy-start(f32[1,16,8192]{2,1,0:T(8,128)} %stack.147) | copy-start | bytes 1572868
  561.6 10.6 %copy-start.33 = (f32[8,16,8192]{2,1,0:T(8,128)S(1)}, f32[8,16,8192]{2,1,0:T(8,128)}, u32[]{:S(2)}) copy-start(f32[8,16,8192]{2,1,0:T(8,128)} %constant_dynamic-update-slice_fusion.40) | copy-start | bytes 12582916
  (108 other events, 450.4 us)

commit v2 on v1

--- a/solution.py
+++ b/solution.py
@@ -15,28 +15,31 @@
     return jnp.einsum(spec, a, b, precision=precision, preferred_element_type=F32)
 
 
-def scan_over_devices(zone, lams, count, place, reverse):
+def scan_over_devices(zone, logs, count, size, reverse):
     sign = -1 if reverse else 1
 
     def shifted(array, step):
         pairs = [(i, i + sign * step) for i in range(count) if 0 <= i + sign * step < count]
         return lax.ppermute(array, "ctx", pairs)
 
-    state = shifted(zone, 1)
-    if count <= 2:
-        return state
-    logs = lams
+    state, gone = shifted(zone, 1), shifted(logs, 1)
     window = 1
     while window < count - 1:
-        ids = jnp.arange(count)
-        if reverse:
-            inside = (ids > place) & (ids <= place + window)
-        else:
-            inside = (ids < place) & (ids >= place - window)
-        weight = jnp.exp(-jnp.sum(jnp.where(inside[:, None, None], logs, 0.0), axis=0))
+        weight = jnp.repeat(jnp.exp(-gone), size, axis=-1)
         state = state + weight[:, :, None] * shifted(state, window)
+        gone = gone + shifted(gone, window)
         window *= 2
     return state
+
+
+def sum_over_devices(array, count):
+    if count & (count - 1):
+        return lax.psum(array, "ctx")
+    step = 1
+    while step < count:
+        array = array + lax.ppermute(array, "ctx", [(i, i ^ step) for i in range(count)])
+        step *= 2
+    return array
 
 
 def per_device(
@@ -48,7 +51,6 @@
     span = min(SPAN, rows)
     blocks = rows // span
     count = lax.axis_size("ctx")
-    place = lax.axis_index("ctx")
     rates = jnp.concatenate([decay_rate, jnp.flip(decay_rate)])
 
     codes = jnp.arange(5, dtype=jnp.int32)
@@ -80,7 +82,7 @@
     expand = (jnp.arange(heads)[:, None] == jnp.arange(width)[None, :] // size).astype(F32)
 
     def wide(array):
-        return jnp.einsum("kth,hw->ktw", array, expand, precision=EXACT)
+        return jnp.einsum("kth,hw->ktw", array, expand, precision=HIGH)
 
     def narrow(array):
         return jnp.einsum("ktw,hw->kth", array, expand, precision=HIGH)
@@ -120,10 +122,9 @@
     af_loc, af_wt, back_f = block_scan(fade_f, ab_f, True)
     ar_loc, ar_wt, back_r = block_scan(fade_r, ab_r, False)
 
-    logs = lax.all_gather(jnp.stack([jnp.sum(tot_f, 0), jnp.sum(tot_r, 0)]), "ctx")
-    logs = columns(logs)
-    ahead = scan_over_devices(jnp.stack([zone_f, back_r]), logs, count, place, False)
-    behind = scan_over_devices(jnp.stack([back_f, zone_r]), logs, count, place, True)
+    logs = jnp.stack([jnp.sum(tot_f, 0), jnp.sum(tot_r, 0)])
+    ahead = scan_over_devices(jnp.stack([zone_f, back_r]), logs, count, size, False)
+    behind = scan_over_devices(jnp.stack([back_f, zone_r]), logs, count, size, True)
 
     def entered(local, weights, entry):
         return jnp.stack([s + w[:, None] * entry for s, w in zip(local, weights)])
@@ -207,7 +208,7 @@
     d_r = (qr + center + xu_r + rates[heads:] * drop_r).reshape(rows, heads)
     grad_s = d_f * slopes[:, :heads] + d_r * slopes[:, heads:]
     own_gain = jnp.sum(both, axis=(0, 1))
-    gains = lax.psum(own_gain + jnp.flip(own_gain), "ctx")
+    gains = sum_over_devices(own_gain + jnp.flip(own_gain), count)
     norm_scale = 1.0 / math.sqrt(rows * count * size)
     return (
         mixed.reshape(rows, width).astype(jnp.bfloat16),

time: 614 us -> 592 us (0.964)
  the two profiles are of different devices: /device:TPU:28 before, /device:TPU:24 now
where the time goes in v2:
time: 592 us; the launch traced here: 580 us
  local copies, waits for them, and re-layouts  173 us (29%)
  waiting for transfers between devices  129 us (22%)
  matrix products  120 us (20%)
  other arithmetic  104 us (18%)
  starting transfers between devices  51.9 us (9%)
    ppermute x18, waiting for transfers between devices, shifted(): return lax.ppermute(array, 'ctx', pairs)  129 us
    dot_general x24, matrix products, ein(): jnp.einsum(spec, a, b, precision=precision, preferred_element_type=F32)  101 us
    another operation x37, local copies, waits for them, and re-layouts, entered(): return jnp.stack([s + w[:, None] * entry for s, w in zip(local, weights)])  63.7 us
    unnamed x351, local copies, waits for them, and re-layouts  62.3 us
    ppermute x18, starting transfers between devices, shifted(): return lax.ppermute(array, 'ctx', pairs)  49.1 us
    unnamed x24, other arithmetic  40.7 us
    add x8, other arithmetic, scan_over_devices(): state = state + weight[:, :, None] * shifted(state, window)  20 us
  transfers between devices with their start and end apart: 22, of which 10 were waited for; matrix products, arithmetic and copies ran while one was open for 33% of the time, Pallas kernels for 0%

profile of v2, /device:TPU:24, one launch (start us, length us, event | category | flops | bytes accessed | tf_op | source)
XLA Modules:
  0.0 580.3 jit_solution(13535615449329927313)
XLA Ops:
  4.1 2.1 add_divide_fusion
  8.5 2.7 collective-permute-start.10
  19.5 2.4 fusion.49
  22.7 2.7 slice_add_fusion
  25.4 2.4 fusion.53
  28.6 2.6 slice_add_fusion.1
  32.4 4.7 collective-permute-start.9
  41.7 3.9 copy.159
  45.6 2.5 copy.175
  48.3 2.4 copy.216
  51.4 14.1 %select_reduce_fusion.2 = (f32[16,8,128]{2,1,0:T(8,128)S(1)}, f32[16,8,128]{2,1,0:T(8,128)S(1)}, f32[16,8,128]{2,1,0:T(8,128)S(1)}, f32[16,8,128]{2,1,0:T(8,128)}, f32[8,128,128]{2,1,0:T(8,128)S(1)}) fusion(f32[16,8,128]{2,1,0:T(8,128)S(1)} %bitcast_add_fusion.4, f32[16,8,128]{2,1,0:T(8,128)S(1)} %bitcast.298, f32[16,8,128]{2,1,0:T(8,128)S(1)} %bitcast.301, ...), kind=kOutput, calls=%fused_computation.14 | convolution fusion | flops 310181888 | bytes 5881856 | tf_op jit(solution)/shard_map/hktp,hksp->hkts/dot_general | solution.py:15
  67.5 8.2 %fusion.57 = f32[8,128,16,64]{1,3,0,2:T(8,128)} fusion(f32[8,128,128]{2,1,0:T(8,128)S(1)} %copy-done.66, f32[16,8,128]{2,1,0:T(8,128)S(1)} %bitcast_add_fusion.4, f32[16,8,128]{2,1,0:T(8,128)S(1)} %bitcast.299, f32[16,8,128]{2,1,0:T(8,128)S(1)} %bitcast.302, f32[16,8,128]{2,1,0:T(8,128)S(1)} %copy.157, f32[16,8,128]{2,1,0:T(8,128)S(1)} %copy.154, ...), kind=kOutput, calls=%fused_computation.79 | convolution fusion | flops 822083584 | bytes 7192576 | tf_op jit(solution)/shard_map/hkts,hktp->hksp/dot_general | solution.py:15
  75.7 3.3 fusion.85
  79.0 2.4 collective-permute-start.12
  86.2 3.0 multiply_add_fusion.3
  89.2 3.4 collective-permute-start.13
  93.9 9.9 %fusion.54 = f32[8,128,16,64]{1,3,0,2:T(8,128)} fusion(f32[8,128,128]{2,1,0:T(8,128)S(1)} %copy-done.67, f32[16,8,128]{2,1,0:T(8,128)S(1)} %copy-done.102, f32[16,8,128]{2,1,0:T(8,128)S(1)} %bitcast.300, f32[16,8,128]{2,1,0:T(8,128)S(1)} %bitcast.303, f32[16,8,128]{2,1,0:T(8,128)S(1)} %copy-done.106, f32[16,8,128]{2,1,0:T(8,128)S(1)} %copy-done.104, ...), kind=kOutput, calls=%fused_computation.78 | convolution fusion | flops 822083584 | bytes 7192576 | tf_op jit(solution)/shard_map/hkts,hksp->hktp/dot_general | solution.py:15
  104.0 12.7 %collective-permute-done.13 = f32[2,1024,128]{2,1,0:T(8,128)} collective-permute-done((f32[2,1024,128]{2,1,0:T(8,128)}, f32[2,1024,128]{2,1,0:T(8,128)}, u32[]{:S(2)}, u32[]{:S(2)}) %collective-permute-start.13) | collective-permute-done | bytes 1048608 | tf_op jit(solution)/shard_map/ppermute | solution.py:23
  116.7 2.8 multiply_add_fusion.2
  119.5 3.7 collective-permute-start.15
  124.5 4.7 copy.161
  129.3 5.4 copy.170
  134.6 4.7 copy.177
  139.4 5.4 copy.178
  149.8 4.6 fusion.51
  156.4 2.8 slice_add_fusion.16
  160.9 2.7 collective-permute-start.19
  167.1 5.4 collective-permute-start.14
  175.9 4.8 collective-permute-start.17
  184.0 3.3 collective-permute-start.16
  189.6 11.9 %collective-permute-done.16 = f32[2,16]{1,0:T(2,128)S(1)} collective-permute-done((f32[2,16]{1,0:T(2,128)S(1)}, f32[2,16]{1,0:T(2,128)S(1)}, u32[]{:S(2)}, u32[]{:S(2)}) %collective-permute-start.16) | collective-permute-done | bytes 160 | tf_op jit(solution)/shard_map/ppermute | solution.py:23
  203.8 2.4 constant_dynamic-update-slice_fusion.23
  208.3 2.4 constant_dynamic-update-slice_fusion.21
  211.7 2.2 constant_dynamic-update-slice_fusion.19
  214.9 2.2 constant_dynamic-update-slice_fusion.17
  217.1 2.6 constant_dynamic-update-slice_fusion.15
  226.2 2.4 fusion.97
  229.9 2.4 fusion.47
  232.4 2.8 slice_add_fusion.24
  245.4 2.5 constant_dynamic-update-slice_fusion.13
  249.9 2.2 constant_dynamic-update-slice_fusion.12
  254.0 2.5 constant_dynamic-update-slice_fusion.11
  258.5 2.2 constant_dynamic-update-slice_fusion.10
  279.6 2.8 collective-permute-start.2
  290.2 28.4 %collective-permute-done.2 = f32[2,1024,128]{2,1,0:T(8,128)} collective-permute-done((f32[2,1024,128]{2,1,0:T(8,128)}, f32[2,1024,128]{2,1,0:T(8,128)}, u32[]{:S(2)}, u32[]{:S(2)}) %collective-permute-start.2) | collective-permute-done | bytes 1048608 | tf_op jit(solution)/shard_map/ppermute | solution.py:23
  318.6 2.9 multiply_add_fusion.7
  328.1 18.5 %collective-permute-done.4 = f32[2,1024,128]{2,1,0:T(8,128)} collective-permute-done((f32[2,1024,128]{2,1,0:T(8,128)}, f32[2,1024,128]{2,1,0:T(8,128)}, u32[]{:S(2)}, u32[]{:S(2)}) %collective-permute-start.4) | collective-permute-done | bytes 1048608 | tf_op jit(solution)/shard_map/ppermute | solution.py:23
  346.6 2.8 multiply_add_fusion.6
  350.8 6.7 %fusion.68 = f32[8,128,128]{2,1,0:T(8,128)} fusion(f32[8,128,128]{2,1,0:T(8,128)S(1)} %copy-done.48, f32[8,1024,128]{2,1,0:T(8,128)} %copy-done.21, f32[8,128,1024]{2,1,0:T(8,128)} %copy-done.10, bf16[8,128,1024]{2,1,0:T(8,128)(2,1)S(1)} %bitcast.267), kind=kOutput, calls=%fused_computation.88 | convolution fusion | flops 807534592 | bytes 11534336 | tf_op jit(solution)/shard_map/ksw,kwn->ksn/dot_general | solution.py:15
  365.2 10.7 %collective-permute-done.6 = f32[2,1024,128]{2,1,0:T(8,128)} collective-permute-done((f32[2,1024,128]{2,1,0:T(8,128)}, f32[2,1024,128]{2,1,0:T(8,128)}, u32[]{:S(2)}, u32[]{:S(2)}) %collective-permute-start.6) | collective-permute-done | bytes 1048608 | tf_op jit(solution)/shard_map/ppermute | solution.py:23
  375.8 2.9 multiply_add_fusion.5
  384.0 44.2 %collective-permute-done.8 = f32[2,1024,128]{2,1,0:T(8,128)} collective-permute-done((f32[2,1024,128]{2,1,0:T(8,128)}, f32[2,1024,128]{2,1,0:T(8,128)}, u32[]{:S(2)}, u32[]{:S(2)}) %collective-permute-start.8) | collective-permute-done | bytes 1048608 | tf_op jit(solution)/shard_map/ppermute | solution.py:23
  434.6 3.4 constant_dynamic-update-slice_fusion.9
  450.4 4.2 fusion.168
  457.2 19.8 %fusion.12 = (bf16[8,128,1024]{2,1,0:T(8,128)(2,1)}, bf16[8,128,1024]{2,1,0:T(8,128)(2,1)}, f32[8,1024,128]{1,2,0:T(8,128)}) fusion(bf16[8,128,1024]{2,1,0:T(8,128)(2,1)S(1)} %bitcast.258, f32[8,128,1024]{2,1,0:T(8,128)} %copy-done.6, f32[8,128,1024]{2,1,0:T(8,128)} %copy.178, f32[8,128,1024]{2,1,0:T(8,128)} %copy-done.10, f32[8,1024,128]{1,2,0:T(8,128)} %copy-done.11, ...), kind=kOutput, calls=%fused_computation.30 | convolution fusion | flops 822083584 | bytes 54792192 | tf_op jit(solution)/shard_map/ksn,kwn->ksw/dot_general | solution.py:15
  477.1 4.2 fusion.10
  483.3 2.5 fusion.96
  520.5 2.8 multiply_reduce_fusion.1
  540.7 2.5 constant_dynamic-update-slice_fusion.37
  550.5 2.9 multiply_reduce_fusion.2
  558.2 3.7 bitcast_add_fusion.2
  564.3 6.0 %fusion.65 = f32[8,128,128]{2,1,0:T(8,128)S(1)} fusion(f32[8,128,128]{2,1,0:T(8,128)} %fusion.171, f32[8,1024,128]{2,1,0:T(8,128)} %copy-done.20, f32[8,128,1024]{2,1,0:T(8,128)} %copy-done.8, bf16[8,128,1024]{2,1,0:T(8,128)(2,1)S(1)} %bitcast.259), kind=kOutput, calls=%fused_computation.85 | convolution fusion | flops 807534592 | bytes 11534336 | tf_op jit(solution)/shard_map/ktw,kwn->ktn/dot_general | solution.py:15
  570.3 5.7 fusion.70
  576.1 3.4 fusion.69
  (563 shorter events, 220.2 us)
Async XLA Ops:
  6.7 11.4 %copy-start.29 = (f32[8,16,128]{1,0,2:T(8,128)}, f32[8,16,128]{1,0,2:T(8,128)S(1)}, u32[]{:S(2)}) copy-start(f32[8,16,128]{1,0,2:T(8,128)S(1)} %copy.167) | copy-start | bytes 196612
  6.8 11.4 %copy-start.107 = (f32[8,16]{1,0:T(8,128)}, f32[8,16]{1,0:T(8,128)S(1)}, u32[]{:S(2)}) copy-start(f32[8,16]{1,0:T(8,128)S(1)} %get-tuple-element.134) | copy-start | bytes 1540
  7.3 10.9 %copy-start.24 = (f32[8,16,128]{1,0,2:T(8,128)}, f32[8,16,128]{1,0,2:T(8,128)S(1)}, u32[]{:S(2)}) copy-start(f32[8,16,128]{1,0,2:T(8,128)S(1)} %copy.162) | copy-start | bytes 196612
  8.5 70.5 %collective-permute-start.10 = (f32[2,16]{1,0:T(2,128)}, f32[2,16]{1,0:T(2,128)}, u32[]{:S(2)}, u32[]{:S(2)}) collective-permute-start(f32[2,16]{1,0:T(2,128)} %pad_maximum_fusion.2), channel_id=1, source_target_pairs={{1,0},{2,1},{3,2},{4,3},{5,4},{6,5},{7,6},{8,7},{9,8},{10,9},{11,1... | collective-permute-start | bytes 392 | tf_op jit(solution)/shard_map/ppermute | solution.py:23
  11.2 154.0 %collective-permute-start.1 = (f32[2,16]{1,0:T(2,128)}, f32[2,16]{1,0:T(2,128)}, u32[]{:S(2)}, u32[]{:S(2)}) collective-permute-start(f32[2,16]{1,0:T(2,128)} %pad_maximum_fusion.2), channel_id=1, source_target_pairs={{0,1},{1,2},{2,3},{3,4},{4,5},{5,6},{6,7},{7,8},{8,9},{9,10},{10,1... | collective-permute-start | bytes 392 | tf_op jit(solution)/shard_map/ppermute | solution.py:23
  15.1 13.5 %copy-start.83 = (f32[1024]{0:T(1024)}, f32[1024]{0:T(1024)S(1)}, u32[]{:S(2)}) copy-start(f32[1024]{0:T(1024)S(1)} %broadcast_in_dim.240) | copy-start | bytes 12292
  15.3 13.2 %copy-start.85 = (f32[1024]{0:T(1024)}, f32[1024]{0:T(1024)S(1)}, u32[]{:S(2)}) copy-start(f32[1024]{0:T(1024)S(1)} %broadcast_in_dim.244) | copy-start | bytes 12292
  15.5 13.1 %copy-start.70 = (f32[1024]{0:T(1024)}, f32[1024]{0:T(1024)S(1)}, u32[]{:S(2)}) copy-start(f32[1024]{0:T(1024)S(1)} %broadcast_in_dim.246) | copy-start | bytes 12292
  15.6 13.0 %copy-start.87 = (f32[1024]{0:T(1024)}, f32[1024]{0:T(1024)S(1)}, u32[]{:S(2)}) copy-start(f32[1024]{0:T(1024)S(1)} %broadcast_in_dim.248) | copy-start | bytes 12292
  15.8 12.0 %copy-start.98 = (f32[1024]{0:T(1024)}, f32[1024]{0:T(1024)S(1)}, u32[]{:S(2)}) copy-start(f32[1024]{0:T(1024)S(1)} %broadcast_in_dim.236) | copy-start | bytes 12292
  15.9 12.7 %copy-start.109 = (f32[1024]{0:T(1024)}, f32[1024]{0:T(1024)S(1)}, u32[]{:S(2)}) copy-start(f32[1024]{0:T(1024)S(1)} %broadcast_in_dim.250) | copy-start | bytes 12292
  32.4 33.0 %collective-permute-start.9 = (f32[2,1024,128]{2,1,0:T(8,128)}, f32[2,1024,128]{2,1,0:T(8,128)}, u32[]{:S(2)}, u32[]{:S(2)}) collective-permute-start(f32[2,1024,128]{2,1,0:T(8,128)} %pad_maximum_fusion.1), channel_id=1, source_target_pairs={{1,0},{2,1},{3,2},{4,3},{5,4},{6,5},{7,6},{8,7},{9,8},{10,9},{11,1... | collective-permute-start | bytes 3145736 | tf_op jit(solution)/shard_map/ppermute | solution.py:23
  39.3 120.9 %collective-permute-start.18 = (f32[16]{0:T(128)}, f32[16]{0:T(128)}, u32[]{:S(2)}, u32[]{:S(2)}) collective-permute-start(f32[16]{0:T(128)} %add.582), channel_id=1, source_target_pairs={{0,1},{1,0},{2,3},{3,2},{4,5},{5,4},{6,7},{7,6},{8,9},{9,8},{10,11... | collective-permute-start | bytes 200 | tf_op jit(solution)/shard_map/ppermute | solution.py:40
  48.2 19.3 %copy-start.101 = (f32[16,8,128]{2,1,0:T(8,128)}, f32[16,8,128]{2,1,0:T(8,128)S(1)}, u32[]{:S(2)}) copy-start(f32[16,8,128]{2,1,0:T(8,128)S(1)} %bitcast_add_fusion.4) | copy-start | bytes 196612
  48.2 19.3 %copy-start.103 = (f32[16,8,128]{2,1,0:T(8,128)}, f32[16,8,128]{2,1,0:T(8,128)S(1)}, u32[]{:S(2)}) copy-start(f32[16,8,128]{2,1,0:T(8,128)S(1)} %copy.154) | copy-start | bytes 196612
  48.3 19.3 %copy-start.105 = (f32[16,8,128]{2,1,0:T(8,128)}, f32[16,8,128]{2,1,0:T(8,128)S(1)}, u32[]{:S(2)}) copy-start(f32[16,8,128]{2,1,0:T(8,128)S(1)} %copy.157) | copy-start | bytes 196612
  50.7 14.7 %copy-start.53 = (bf16[128,8,8,128]{3,2,1,0:T(8,128)(2,1)}, bf16[128,8,8,128]{3,2,1,0:T(8,128)(2,1)S(1)}, u32[]{:S(2)}) copy-start(bf16[128,8,8,128]{3,2,1,0:T(8,128)(2,1)S(1)} %copy.216) | copy-start | bytes 6291460
  65.4 10.3 %copy-start.65 = (f32[8,128,16]{2,0,1:T(8,128)S(1)}, f32[8,128,16]{2,0,1:T(8,128)}, u32[]{:S(2)}) copy-start(f32[8,128,16]{2,0,1:T(8,128)} %get-tuple-element.136) | copy-start | bytes 196612
  65.4 20.7 %collective-permute-start.11 = (f32[2,1024,128]{2,1,0:T(8,128)}, f32[2,1024,128]{2,1,0:T(8,128)}, u32[]{:S(2)}, u32[]{:S(2)}) collective-permute-start(f32[2,1024,128]{2,1,0:T(8,128)} %collective-permute-done.9), channel_id=1, source_target_pairs={{1,0},{2,1},{3,2},{4,3},{5,4},{6,5},{7,6},{8,7},{9,8},{10,9},{11,1... | collective-permute-start | bytes 3145736 | tf_op jit(solution)/shard_map/ppermute | solution.py:23
  79.0 3.9 collective-permute-start.12
  89.2 27.5 %collective-permute-start.13 = (f32[2,1024,128]{2,1,0:T(8,128)}, f32[2,1024,128]{2,1,0:T(8,128)}, u32[]{:S(2)}, u32[]{:S(2)}) collective-permute-start(f32[2,1024,128]{2,1,0:T(8,128)} %multiply_add_fusion.3), channel_id=1, source_target_pairs={{2,0},{3,1},{4,2},{5,3},{6,4},{7,5},{8,6},{9,7},{10,8},{11,9},{12,... | collective-permute-start | bytes 3145736 | tf_op jit(solution)/shard_map/ppermute | solution.py:23
  119.5 54.4 %collective-permute-start.15 = (f32[2,1024,128]{2,1,0:T(8,128)}, f32[2,1024,128]{2,1,0:T(8,128)}, u32[]{:S(2)}, u32[]{:S(2)}) collective-permute-start(f32[2,1024,128]{2,1,0:T(8,128)} %multiply_add_fusion.2), channel_id=1, source_target_pairs={{4,0},{5,1},{6,2},{7,3},{8,4},{9,5},{10,6},{11,7},{12,8},{13,9},{1... | collective-permute-start | bytes 3145736 | tf_op jit(solution)/shard_map/ppermute | solution.py:23
  154.4 12.7 %copy-start.152 = (f32[2,16]{1,0:T(2,128)S(1)}, f32[2,16]{1,0:T(2,128)}, u32[]{:S(2)}) copy-start(f32[2,16]{1,0:T(2,128)} %get-tuple-element.100) | copy-start | bytes 388
  159.2 44.6 %copy-start.88 = (f32[1024]{0:T(1024)S(1)}, f32[1024]{0:T(1024)}, u32[]{:S(2)}) copy-start(f32[1024]{0:T(1024)} %copy-done.87) | copy-start | bytes 12292
  159.2 44.6 %copy-start.143 = (f32[1024]{0:T(1024)S(1)}, f32[1024]{0:T(1024)}, u32[]{:S(2)}) copy-start(f32[1024]{0:T(1024)} %get-tuple-element.25) | copy-start | bytes 12292
  160.9 4.3 collective-permute-start.19
  165.2 7.3 %collective-permute-start.20 = (f32[16]{0:T(128)S(1)}, f32[16]{0:T(128)S(1)}, u32[]{:S(2)}, u32[]{:S(2)}) collective-permute-start(f32[16]{0:T(128)S(1)} %add.584), channel_id=1, source_target_pairs={{0,4},{1,5},{2,6},{3,7},{4,0},{5,1},{6,2},{7,3},{8,12},{9,13},{10,... | collective-permute-start | bytes 200 | tf_op jit(solution)/shard_map/ppermute | solution.py:40
  165.2 15.5 %collective-permute-start.3 = (f32[2,16]{1,0:T(2,128)}, f32[2,16]{1,0:T(2,128)S(1)}, u32[]{:S(2)}, u32[]{:S(2)}) collective-permute-start(f32[2,16]{1,0:T(2,128)} %collective-permute-done.1), channel_id=1, source_target_pairs={{0,1},{1,2},{2,3},{3,4},{4,5},{5,6},{6,7},{7,8},{8,9},{9,10},{10,1... | collective-permute-start | bytes 392 | tf_op jit(solution)/shard_map/ppermute | solution.py:23
  167.1 6.7 %collective-permute-start.14 = (f32[2,16]{1,0:T(2,128)S(1)}, f32[2,16]{1,0:T(2,128)S(1)}, u32[]{:S(2)}, u32[]{:S(2)}) collective-permute-start(f32[2,16]{1,0:T(2,128)S(1)} %copy-done.152), channel_id=1, source_target_pairs={{2,0},{3,1},{4,2},{5,3},{6,4},{7,5},{8,6},{9,7},{10,8},{11,9},{12,... | collective-permute-start | bytes 392 | tf_op jit(solution)/shard_map/ppermute | solution.py:23
  172.5 11.0 %collective-permute-start.21 = (f32[16]{0:T(128)S(1)}, f32[16]{0:T(128)S(1)}, u32[]{:S(2)}, u32[]{:S(2)}) collective-permute-start(f32[16]{0:T(128)S(1)} %add.585), channel_id=1, source_target_pairs={{0,8},{1,9},{2,10},{3,11},{4,12},{5,13},{6,14},{7,15},{8,0},{9,1},... | collective-permute-start | bytes 200 | tf_op jit(solution)/shard_map/ppermute | solution.py:40
  173.9 32.3 %copy-start.142 = (f32[1024]{0:T(1024)S(1)}, f32[1024]{0:T(1024)}, u32[]{:S(2)}) copy-start(f32[1024]{0:T(1024)} %get-tuple-element.26) | copy-start | bytes 12292
  175.8 26.0 %copy-start.46 = (f32[2,1024,128]{2,1,0:T(8,128)}, f32[2,1024,128]{2,1,0:T(8,128)S(1)}, u32[]{:S(2)}) copy-start(f32[2,1024,128]{2,1,0:T(8,128)S(1)} %multiply_add_fusion.1) | copy-start | bytes 3145732
  175.8 32.4 %copy-start.86 = (f32[1024]{0:T(1024)S(1)}, f32[1024]{0:T(1024)}, u32[]{:S(2)}) copy-start(f32[1024]{0:T(1024)} %copy-done.85) | copy-start | bytes 12292
  175.9 32.4 %copy-start.141 = (f32[1024]{0:T(1024)S(1)}, f32[1024]{0:T(1024)}, u32[]{:S(2)}) copy-start(f32[1024]{0:T(1024)} %get-tuple-element.27) | copy-start | bytes 12292
  175.9 26.0 %collective-permute-start.17 = (f32[2,1024,128]{2,1,0:T(8,128)S(1)}, f32[2,1024,128]{2,1,0:T(8,128)}, u32[]{:S(2)}, u32[]{:S(2)}) collective-permute-start(f32[2,1024,128]{2,1,0:T(8,128)S(1)} %multiply_add_fusion.1), channel_id=1, source_target_pairs={{8,0},{9,1},{10,2},{11,3},{12,4},{13,5},{14,6},{15,7},{24,16},{25,... | collective-permute-start | bytes 3145736 | tf_op jit(solution)/shard_map/ppermute | solution.py:23
  181.6 6.4 %collective-permute-start.5 = (f32[2,16]{1,0:T(2,128)S(1)}, f32[2,16]{1,0:T(2,128)S(1)}, u32[]{:S(2)}, u32[]{:S(2)}) collective-permute-start(f32[2,16]{1,0:T(2,128)S(1)} %get-tuple-element.74), channel_id=1, source_target_pairs={{0,2},{1,3},{2,4},{3,5},{4,6},{5,7},{6,8},{7,9},{8,10},{9,11},{10,... | collective-permute-start | bytes 392 | tf_op jit(solution)/shard_map/ppermute | solution.py:23
  184.0 17.5 %collective-permute-start.16 = (f32[2,16]{1,0:T(2,128)S(1)}, f32[2,16]{1,0:T(2,128)S(1)}, u32[]{:S(2)}, u32[]{:S(2)}) collective-permute-start(f32[2,16]{1,0:T(2,128)S(1)} %get-tuple-element.98), channel_id=1, source_target_pairs={{4,0},{5,1},{6,2},{7,3},{8,4},{9,5},{10,6},{11,7},{12,8},{13,9},{1... | collective-permute-start | bytes 392 | tf_op jit(solution)/shard_map/ppermute | solution.py:23
  188.1 13.6 %collective-permute-start.7 = (f32[2,16]{1,0:T(2,128)S(1)}, f32[2,16]{1,0:T(2,128)S(1)}, u32[]{:S(2)}, u32[]{:S(2)}) collective-permute-start(f32[2,16]{1,0:T(2,128)S(1)} %get-tuple-element.72), channel_id=1, source_target_pairs={{0,4},{1,5},{2,6},{3,7},{4,8},{5,9},{6,10},{7,11},{8,12},{9,13},{1... | collective-permute-start | bytes 392 | tf_op jit(solution)/shard_map/ppermute | solution.py:23
  236.3 43.4 %collective-permute-start = (f32[2,1024,128]{2,1,0:T(8,128)}, f32[2,1024,128]{2,1,0:T(8,128)}, u32[]{:S(2)}, u32[]{:S(2)}) collective-permute-start(f32[2,1024,128]{2,1,0:T(8,128)} %pad_maximum_fusion), channel_id=1, source_target_pairs={{0,1},{1,2},{2,3},{3,4},{4,5},{5,6},{6,7},{7,8},{8,9},{9,10},{10,1... | collective-permute-start | bytes 3145736 | tf_op jit(solution)/shard_map/ppermute | solution.py:23
  238.4 11.5 %copy-start.134 = (f32[1024]{0:T(1024)S(1)}, f32[1024]{0:T(1024)}, u32[]{:S(2)}) copy-start(f32[1024]{0:T(1024)} %get-tuple-element.153) | copy-start | bytes 12292
  243.5 10.5 %copy-start.77 = (f32[1024]{0:T(1024)S(1)}, f32[1024]{0:T(1024)}, u32[]{:S(2)}) copy-start(f32[1024]{0:T(1024)} %copy-done.75) | copy-start | bytes 12292
  243.5 10.5 %copy-start.133 = (f32[1024]{0:T(1024)S(1)}, f32[1024]{0:T(1024)}, u32[]{:S(2)}) copy-start(f32[1024]{0:T(1024)} %get-tuple-element.154) | copy-start | bytes 12292
  247.9 10.6 %copy-start.132 = (f32[1024]{0:T(1024)S(1)}, f32[1024]{0:T(1024)}, u32[]{:S(2)}) copy-start(f32[1024]{0:T(1024)} %get-tuple-element.155) | copy-start | bytes 12292
  279.6 38.9 %collective-permute-start.2 = (f32[2,1024,128]{2,1,0:T(8,128)}, f32[2,1024,128]{2,1,0:T(8,128)}, u32[]{:S(2)}, u32[]{:S(2)}) collective-permute-start(f32[2,1024,128]{2,1,0:T(8,128)} %collective-permute-done), channel_id=1, source_target_pairs={{0,1},{1,2},{2,3},{3,4},{4,5},{5,6},{6,7},{7,8},{8,9},{9,10},{10,1... | collective-permute-start | bytes 3145736 | tf_op jit(solution)/shard_map/ppermute | solution.py:23
  288.2 35.1 %copy-start.64 = (f32[1,16,8192]{2,1,0:T(8,128)S(1)}, f32[1,16,8192]{2,1,0:T(8,128)}, u32[]{:S(2)}) copy-start(f32[1,16,8192]{2,1,0:T(8,128)} %stack.153) | copy-start | bytes 1572868
  321.4 25.2 %collective-permute-start.4 = (f32[2,1024,128]{2,1,0:T(8,128)}, f32[2,1024,128]{2,1,0:T(8,128)}, u32[]{:S(2)}, u32[]{:S(2)}) collective-permute-start(f32[2,1024,128]{2,1,0:T(8,128)} %multiply_add_fusion.7), channel_id=1, source_target_pairs={{0,2},{1,3},{2,4},{3,5},{4,6},{5,7},{6,8},{7,9},{8,10},{9,11},{10,... | collective-permute-start | bytes 3145736 | tf_op jit(solution)/shard_map/ppermute | solution.py:23
  326.1 24.6 %copy-start.4 = (bf16[1024,1024]{1,0:T(8,128)(2,1)S(1)}, bf16[1024,1024]{1,0:T(8,128)(2,1)}, u32[]{:S(2)}) copy-start(bf16[1024,1024]{1,0:T(8,128)(2,1)} %param.10) | copy-start | bytes 6291460
  326.1 24.6 %copy-start.48 = (f32[8,128,128]{2,1,0:T(8,128)S(1)}, f32[8,128,128]{2,1,0:T(8,128)}, u32[]{:S(2)}) copy-start(f32[8,128,128]{2,1,0:T(8,128)} %fusion.170) | copy-start | bytes 1572868
  349.5 26.4 %collective-permute-start.6 = (f32[2,1024,128]{2,1,0:T(8,128)}, f32[2,1024,128]{2,1,0:T(8,128)}, u32[]{:S(2)}, u32[]{:S(2)}) collective-permute-start(f32[2,1024,128]{2,1,0:T(8,128)} %multiply_add_fusion.6), channel_id=1, source_target_pairs={{0,4},{1,5},{2,6},{3,7},{4,8},{5,9},{6,10},{7,11},{8,12},{9,13},{1... | collective-permute-start | bytes 3145736 | tf_op jit(solution)/shard_map/ppermute | solution.py:23
  363.2 16.7 %copy-start.49 = (f32[8,128,16]{2,0,1:T(8,128)S(1)}, f32[8,128,16]{2,0,1:T(8,128)}, u32[]{:S(2)}) copy-start(f32[8,128,16]{2,0,1:T(8,128)} %get-tuple-element.115) | copy-start | bytes 196612
  365.1 65.0 %copy-start.97 = (f32[1024]{0:T(1024)S(1)}, f32[1024]{0:T(1024)}, u32[]{:S(2)}) copy-start(f32[1024]{0:T(1024)} %copy-done.96) | copy-start | bytes 12292
  365.1 65.0 %copy-start.114 = (f32[1024]{0:T(1024)S(1)}, f32[1024]{0:T(1024)}, u32[]{:S(2)}) copy-start(f32[1024]{0:T(1024)} %get-tuple-element.161) | copy-start | bytes 12292
  378.7 49.5 %collective-permute-start.8 = (f32[2,1024,128]{2,1,0:T(8,128)}, f32[2,1024,128]{2,1,0:T(8,128)}, u32[]{:S(2)}, u32[]{:S(2)}) collective-permute-start(f32[2,1024,128]{2,1,0:T(8,128)} %multiply_add_fusion.5), channel_id=1, source_target_pairs={{0,8},{1,9},{2,10},{3,11},{4,12},{5,13},{6,14},{7,15},{16,24},{17,... | collective-permute-start | bytes 3145736 | tf_op jit(solution)/shard_map/ppermute | solution.py:23
  380.0 51.4 %copy-start.130 = (f32[1024]{0:T(1024)S(1)}, f32[1024]{0:T(1024)}, u32[]{:S(2)}) copy-start(f32[1024]{0:T(1024)} %get-tuple-element.38) | copy-start | bytes 12292
  382.0 48.2 %copy-start.19 = (f32[8,1024,128]{2,1,0:T(8,128)S(1)}, f32[8,1024,128]{2,1,0:T(8,128)}, u32[]{:S(2)}) copy-start(f32[8,1024,128]{2,1,0:T(8,128)} %copy-done.18) | copy-start | bytes 12582916
  382.0 49.4 %copy-start.36 = (f32[1,1024,128]{2,1,0:T(8,128)S(1)}, f32[1,1024,128]{2,1,0:T(8,128)}, u32[]{:S(2)}) copy-start(f32[1,1024,128]{2,1,0:T(8,128)} %get-tuple-element.82) | copy-start | bytes 1572868
  384.0 48.4 %copy-start.74 = (f32[1024]{0:T(1024)S(1)}, f32[1024]{0:T(1024)}, u32[]{:S(2)}) copy-start(f32[1024]{0:T(1024)} %copy-done.72) | copy-start | bytes 12292
  384.0 48.4 %copy-start.129 = (f32[1024]{0:T(1024)S(1)}, f32[1024]{0:T(1024)}, u32[]{:S(2)}) copy-start(f32[1024]{0:T(1024)} %get-tuple-element.37) | copy-start | bytes 12292
  485.8 12.7 %copy-start.51 = (f32[1,1024,128]{2,1,0:T(8,128)S(1)}, f32[1,1024,128]{2,1,0:T(8,128)}, u32[]{:S(2)}) copy-start(f32[1,1024,128]{2,1,0:T(8,128)} %get-tuple-element.46) | copy-start | bytes 1572868
  508.2 11.5 %copy-start.59 = (f32[1,16,8192]{2,1,0:T(8,128)S(1)}, f32[1,16,8192]{2,1,0:T(8,128)}, u32[]{:S(2)}) copy-start(f32[1,16,8192]{2,1,0:T(8,128)} %stack.174) | copy-start | bytes 1572868
  508.2 12.3 %copy-start.32 = (f32[8,16,8192]{2,1,0:T(8,128)S(1)}, f32[8,16,8192]{2,1,0:T(8,128)}, u32[]{:S(2)}) copy-start(f32[8,16,8192]{2,1,0:T(8,128)} %constant_dynamic-update-slice_fusion.50) | copy-start | bytes 12582916
  508.2 12.3 %copy-start.58 = (f32[1,16,8192]{2,1,0:T(8,128)S(1)}, f32[1,16,8192]{2,1,0:T(8,128)}, u32[]{:S(2)}) copy-start(f32[1,16,8192]{2,1,0:T(8,128)} %stack.164) | copy-start | bytes 1572868
  508.2 12.3 %copy-start.55 = (f32[1,16,8192]{2,1,0:T(8,128)S(1)}, f32[1,16,8192]{2,1,0:T(8,128)}, u32[]{:S(2)}) copy-start(f32[1,16,8192]{2,1,0:T(8,128)} %stack.165) | copy-start | bytes 1572868
  539.9 10.6 %copy-start.33 = (f32[8,16,8192]{2,1,0:T(8,128)S(1)}, f32[8,16,8192]{2,1,0:T(8,128)}, u32[]{:S(2)}) copy-start(f32[8,16,8192]{2,1,0:T(8,128)} %constant_dynamic-update-slice_fusion.40) | copy-start | bytes 12582916
  (115 other events, 617.6 us)
